TPU v7x, 512 devices: a whole 4x8x8 slice. The times are simulated.
512 devices in a mesh: blk: 64 (over z, y_lo, core), rep: 8 (over y_hi, x).
Axes of the slice: x: 4, y: 8 (y_hi: 2, y_lo: 4; y = y_hi * 4 + y_lo), z: 8, core: 2. Of those that a mesh axis runs over, the one named last changes fastest.
Arguments:
- points: float32 [16, 81920], P(None, ('blk', 'rep')), may hold values from -3 to 3
- vectors: float32 [32, 81920], P(None, ('blk', 'rep')), may hold values from -1.2 to 1.2
- lengthscales: float32 [16], replicated, may hold values from 0.6 to 1.6
Outputs:
- product: float32 [32, 81920], P(None, ('blk', 'rep'))
All inputs are finite; a program needn't handle non-finite values.
Results may differ from a plain program's by a relative error of at most 0.0003.
Values sent between devices are 32-bit elements; how exact they have to be, the bound alone decides.
A program may use at most 64 MiB of HBM per device.

v0:
```python
import jax
import jax.numpy as jnp
from jax import lax
from jax.sharding import PartitionSpec as P


def shifted(value, axis, steps):
    count = lax.axis_size(axis)
    pairs = [(source, (source + steps) % count) for source in range(count)]
    return lax.ppermute(value, axis, pairs)


def matern_tile(col_z, row_z, row_sq):
    col_sq = jnp.sum(col_z * col_z, axis=0)
    cross = lax.dot_general(
        col_z,
        row_z,
        (((0,), (0,)), ((), ())),
        precision=lax.Precision.HIGHEST,
        preferred_element_type=jnp.float32,
    )
    sqdist = jnp.maximum(col_sq[:, None] + row_sq[None, :] - 2.0 * cross, 0.0)
    svalue = jnp.sqrt(5.0 * sqdist)
    return (1.0 + svalue + svalue * svalue / 3.0) * jnp.exp(-svalue)


def rows_times(col_v, kernel):
    return lax.dot(
        col_v, kernel, precision=lax.Precision.HIGHEST, preferred_element_type=jnp.float32
    )


def cols_times(row_v, kernel):
    return lax.dot_general(
        row_v,
        kernel,
        (((1,), (1,)), ((), ())),
        precision=lax.Precision.HIGHEST,
        preferred_element_type=jnp.float32,
    )


def per_device(points, vectors, lengthscales):
    local_z = points / lengthscales[:, None]
    row_z, row_v = (
        lax.all_gather(local_z, "rep", axis=1, tiled=True),
        lax.all_gather(vectors, "rep", axis=1, tiled=True),
    )
    row_sq = jnp.sum(row_z * row_z, axis=0)
    half = lax.axis_size("blk") // 2
    row_acc = rows_times(vectors, matern_tile(local_z, row_z, row_sq))

    def cycle_step(step, carry):
        col_z, col_v, travel, row_total = carry
        col_z, col_v, travel = shifted((col_z, col_v, travel), "blk", 1)
        kernel = matern_tile(col_z, row_z, row_sq)
        return (
            col_z,
            col_v,
            travel + cols_times(row_v, kernel),
            row_total + rows_times(col_v, kernel),
        )

    start = (local_z, vectors, jnp.zeros_like(vectors), row_acc)
    col_z, col_v, travel, row_acc = lax.fori_loop(1, half, cycle_step, start)
    col_z, col_v = shifted((col_z, col_v), "blk", 1)
    returned = shifted(travel, "blk", 1 - half)
    row_acc = row_acc + rows_times(col_v, matern_tile(col_z, row_z, row_sq))
    return lax.psum_scatter(row_acc, "rep", scatter_dimension=1, tiled=True) + returned


def solution(mesh):
    return jax.shard_map(
        per_device,
        mesh=mesh,
        in_specs=(P(None, ("blk", "rep")), P(None, ("blk", "rep")), P()),
        out_specs=P(None, ("blk", "rep")),
        check_vma=False,
    )
```

profile of v0, /device:TPU:1, one launch (start us, length us, event | category | flops | bytes accessed | tf_op | source)
XLA Modules:
  0.0 663.8 jit_solution(17798006925289154229)
XLA Ops:
  8.1 39.1 %all-gather = f32[8,160,16]{1,2,0:T(8,128)S(1)} all-gather(f32[1,160,16]{1,2,0:T(8,128)S(1)} %bitcast.59), channel_id=1, replica_groups=mesh['blk'=64,'rep'=8] {'rep'}, dimensions={0}, use_global_device_ids=true | all-gather | bytes 92160 | tf_op jit(solution)/shard_map/all_gather | solution.py:46
  49.2 37.7 %all-gather.1 = f32[8,160,32]{1,2,0:T(8,128)S(1)} all-gather(f32[1,160,32]{1,2,0:T(8,128)S(1)} %bitcast.57), channel_id=1, replica_groups=mesh['blk'=64,'rep'=8] {'rep'}, dimensions={0}, use_global_device_ids=true | all-gather | bytes 184320 | tf_op jit(solution)/shard_map/all_gather | solution.py:47
  87.1 460.5 %while.17 = (s32[]{:T(128)}, f32[16,160]{1,0:T(8,128)S(1)}, f32[32,160]{1,0:T(8,128)S(1)}, f32[32,160]{1,0:T(8,128)S(1)}, f32[32,1280]{1,0:T(8,128)S(1)}, /*inde...) while((s32[]{:T(128)}, f32[16,160]{1,0:T(8,128)S(1)}, ...), condition=%wide.region_4.0_spmd.clone, body=%wide.region_2.0_spmd.clone.sunk | while | flops 198916960 | bytes 3426791 | solution.py:65
  87.2 15.8 %collective-permute-start = (f32[16,160]{1,0:T(8,128)S(1)}, f32[16,160]{1,0:T(8,128)S(1)}, u32[]{:S(2)}, u32[]{:S(2)}) collective-permute-start(f32[16,160]{1,0:T(8,128)S(1)} %get-tuple-element.159), channel_id=1, source_target_pairs={{0,8},{8,16},{16,24},{24,32},{32,40},{40,48},{48,56},{56,64},{64,7... | collective-permute-start | bytes 30728 | tf_op jit(solution)/shard_map/while/body/eval_jaxpr/ppermute | solution.py:10
  104.9 3.6 collective-permute-start.1
  117.2 3.5 collective-permute-start.1
  123.4 2.6 collective-permute-done.1
  131.4 2.7 collective-permute-start.1
  148.4 2.7 collective-permute-done
  152.4 2.6 collective-permute-done.1
  162.3 3.3 collective-permute-done
  166.9 2.6 collective-permute-done.1
  176.8 3.3 collective-permute-done
  181.4 2.6 collective-permute-done.1
  191.3 3.3 collective-permute-done
  195.9 2.6 collective-permute-done.1
  205.7 3.3 collective-permute-done
  220.2 3.3 collective-permute-done
  224.8 2.6 collective-permute-done.1
  234.7 3.3 collective-permute-done
  239.3 2.6 collective-permute-done.1
  249.2 3.3 collective-permute-done
  253.8 2.6 collective-permute-done.1
  263.7 3.3 collective-permute-done
  268.3 2.6 collective-permute-done.1
  278.2 3.3 collective-permute-done
  282.8 2.6 collective-permute-done.1
  292.7 3.3 collective-permute-done
  297.3 2.6 collective-permute-done.1
  307.2 3.3 collective-permute-done
  311.8 2.6 collective-permute-done.1
  321.6 3.3 collective-permute-done
  326.2 2.6 collective-permute-done.1
  336.1 3.3 collective-permute-done
  340.7 2.6 collective-permute-done.1
  350.6 3.3 collective-permute-done
  355.2 2.6 collective-permute-done.1
  365.1 3.3 collective-permute-done
  369.7 2.6 collective-permute-done.1
  379.6 3.3 collective-permute-done
  384.2 2.6 collective-permute-done.1
  394.1 3.3 collective-permute-done
  398.7 2.6 collective-permute-done.1
  408.6 3.3 collective-permute-done
  413.2 2.6 collective-permute-done.1
  423.1 3.3 collective-permute-done
  437.5 3.3 collective-permute-done
  442.1 2.6 collective-permute-done.1
  452.0 3.3 collective-permute-done
  456.6 2.6 collective-permute-done.1
  466.5 3.3 collective-permute-done
  471.1 2.6 collective-permute-done.1
  481.0 3.3 collective-permute-done
  485.6 2.6 collective-permute-done.1
  495.5 3.3 collective-permute-done
  510.0 3.3 collective-permute-done
  514.6 2.6 collective-permute-done.1
  524.5 3.3 collective-permute-done
  529.1 2.6 collective-permute-done.1
  539.0 3.3 collective-permute-done
  543.6 2.6 collective-permute-done.1
  551.5 5.3 collective-permute-done.4
  561.0 2.9 collective-permute-start.5
  563.9 91.5 %reduce-scatter.4.cloned.1.call-done = f32[160,32]{1,0:T(8,128)} async-done(((f32[1280,32]{1,0:T(8,128)}), f32[160,32]{1,0:T(8,128)}) %reduce-scatter.4.cloned.1.call-update) | async-done | bytes 20496
  (371 shorter events, 285.2 us)
Async XLA Ops:
  6.5 648.8 %reduce-scatter.4.cloned.1.call-start = ((), (), s32[]{:S(2)}) async-start(), calls=%async_computation.1 | async-start | bytes 737280
  87.2 21.3 %collective-permute-start = (f32[16,160]{1,0:T(8,128)S(1)}, f32[16,160]{1,0:T(8,128)S(1)}, u32[]{:S(2)}, u32[]{:S(2)}) collective-permute-start(f32[16,160]{1,0:T(8,128)S(1)} %get-tuple-element.159), channel_id=1, source_target_pairs={{0,8},{8,16},{16,24},{24,32},{32,40},{40,48},{48,56},{56,64},{64,7... | collective-permute-start | bytes 30728 | tf_op jit(solution)/shard_map/while/body/eval_jaxpr/ppermute | solution.py:10
  103.0 9.2 %collective-permute-start.2 = (f32[32,160]{1,0:T(8,128)S(1)}, f32[32,160]{1,0:T(8,128)S(1)}, u32[]{:S(2)}, u32[]{:S(2)}) collective-permute-start(f32[32,160]{1,0:T(8,128)S(1)} %broadcast_select_fusion.2), channel_id=1, source_target_pairs={{0,8},{8,16},{16,24},{24,32},{32,40},{40,48},{48,56},{56,64},{64,7... | collective-permute-start | bytes 61448 | tf_op jit(solution)/shard_map/while/body/eval_jaxpr/ppermute | solution.py:10
  115.2 11.4 %collective-permute-start.2 = (f32[32,160]{1,0:T(8,128)S(1)}, f32[32,160]{1,0:T(8,128)S(1)}, u32[]{:S(2)}, u32[]{:S(2)}) collective-permute-start(f32[32,160]{1,0:T(8,128)S(1)} %broadcast_select_fusion.2), channel_id=1, source_target_pairs={{0,8},{8,16},{16,24},{24,32},{32,40},{40,48},{48,56},{56,64},{64,7... | collective-permute-start | bytes 61448 | tf_op jit(solution)/shard_map/while/body/eval_jaxpr/ppermute | solution.py:10
  129.4 11.7 %collective-permute-start.2 = (f32[32,160]{1,0:T(8,128)S(1)}, f32[32,160]{1,0:T(8,128)S(1)}, u32[]{:S(2)}, u32[]{:S(2)}) collective-permute-start(f32[32,160]{1,0:T(8,128)S(1)} %broadcast_select_fusion.2), channel_id=1, source_target_pairs={{0,8},{8,16},{16,24},{24,32},{32,40},{40,48},{48,56},{56,64},{64,7... | collective-permute-start | bytes 61448 | tf_op jit(solution)/shard_map/while/body/eval_jaxpr/ppermute | solution.py:10
  131.4 9.1 %collective-permute-start.1 = (f32[32,160]{1,0:T(8,128)S(1)}, f32[32,160]{1,0:T(8,128)S(1)}, u32[]{:S(2)}, u32[]{:S(2)}) collective-permute-start(f32[32,160]{1,0:T(8,128)S(1)} %get-tuple-element.160), channel_id=1, source_target_pairs={{0,8},{8,16},{16,24},{24,32},{32,40},{40,48},{48,56},{56,64},{64,7... | collective-permute-start | bytes 61448 | tf_op jit(solution)/shard_map/while/body/eval_jaxpr/ppermute | solution.py:10
  143.9 11.7 %collective-permute-start.2 = (f32[32,160]{1,0:T(8,128)S(1)}, f32[32,160]{1,0:T(8,128)S(1)}, u32[]{:S(2)}, u32[]{:S(2)}) collective-permute-start(f32[32,160]{1,0:T(8,128)S(1)} %broadcast_select_fusion.2), channel_id=1, source_target_pairs={{0,8},{8,16},{16,24},{24,32},{32,40},{40,48},{48,56},{56,64},{64,7... | collective-permute-start | bytes 61448 | tf_op jit(solution)/shard_map/while/body/eval_jaxpr/ppermute | solution.py:10
  145.9 9.1 %collective-permute-start.1 = (f32[32,160]{1,0:T(8,128)S(1)}, f32[32,160]{1,0:T(8,128)S(1)}, u32[]{:S(2)}, u32[]{:S(2)}) collective-permute-start(f32[32,160]{1,0:T(8,128)S(1)} %get-tuple-element.160), channel_id=1, source_target_pairs={{0,8},{8,16},{16,24},{24,32},{32,40},{40,48},{48,56},{56,64},{64,7... | collective-permute-start | bytes 61448 | tf_op jit(solution)/shard_map/while/body/eval_jaxpr/ppermute | solution.py:10
  158.4 11.7 %collective-permute-start.2 = (f32[32,160]{1,0:T(8,128)S(1)}, f32[32,160]{1,0:T(8,128)S(1)}, u32[]{:S(2)}, u32[]{:S(2)}) collective-permute-start(f32[32,160]{1,0:T(8,128)S(1)} %broadcast_select_fusion.2), channel_id=1, source_target_pairs={{0,8},{8,16},{16,24},{24,32},{32,40},{40,48},{48,56},{56,64},{64,7... | collective-permute-start | bytes 61448 | tf_op jit(solution)/shard_map/while/body/eval_jaxpr/ppermute | solution.py:10
  160.4 9.1 %collective-permute-start.1 = (f32[32,160]{1,0:T(8,128)S(1)}, f32[32,160]{1,0:T(8,128)S(1)}, u32[]{:S(2)}, u32[]{:S(2)}) collective-permute-start(f32[32,160]{1,0:T(8,128)S(1)} %get-tuple-element.160), channel_id=1, source_target_pairs={{0,8},{8,16},{16,24},{24,32},{32,40},{40,48},{48,56},{56,64},{64,7... | collective-permute-start | bytes 61448 | tf_op jit(solution)/shard_map/while/body/eval_jaxpr/ppermute | solution.py:10
  172.9 11.7 %collective-permute-start.2 = (f32[32,160]{1,0:T(8,128)S(1)}, f32[32,160]{1,0:T(8,128)S(1)}, u32[]{:S(2)}, u32[]{:S(2)}) collective-permute-start(f32[32,160]{1,0:T(8,128)S(1)} %broadcast_select_fusion.2), channel_id=1, source_target_pairs={{0,8},{8,16},{16,24},{24,32},{32,40},{40,48},{48,56},{56,64},{64,7... | collective-permute-start | bytes 61448 | tf_op jit(solution)/shard_map/while/body/eval_jaxpr/ppermute | solution.py:10
  174.8 9.1 %collective-permute-start.1 = (f32[32,160]{1,0:T(8,128)S(1)}, f32[32,160]{1,0:T(8,128)S(1)}, u32[]{:S(2)}, u32[]{:S(2)}) collective-permute-start(f32[32,160]{1,0:T(8,128)S(1)} %get-tuple-element.160), channel_id=1, source_target_pairs={{0,8},{8,16},{16,24},{24,32},{32,40},{40,48},{48,56},{56,64},{64,7... | collective-permute-start | bytes 61448 | tf_op jit(solution)/shard_map/while/body/eval_jaxpr/ppermute | solution.py:10
  187.4 11.7 %collective-permute-start.2 = (f32[32,160]{1,0:T(8,128)S(1)}, f32[32,160]{1,0:T(8,128)S(1)}, u32[]{:S(2)}, u32[]{:S(2)}) collective-permute-start(f32[32,160]{1,0:T(8,128)S(1)} %broadcast_select_fusion.2), channel_id=1, source_target_pairs={{0,8},{8,16},{16,24},{24,32},{32,40},{40,48},{48,56},{56,64},{64,7... | collective-permute-start | bytes 61448 | tf_op jit(solution)/shard_map/while/body/eval_jaxpr/ppermute | solution.py:10
  189.3 9.1 %collective-permute-start.1 = (f32[32,160]{1,0:T(8,128)S(1)}, f32[32,160]{1,0:T(8,128)S(1)}, u32[]{:S(2)}, u32[]{:S(2)}) collective-permute-start(f32[32,160]{1,0:T(8,128)S(1)} %get-tuple-element.160), channel_id=1, source_target_pairs={{0,8},{8,16},{16,24},{24,32},{32,40},{40,48},{48,56},{56,64},{64,7... | collective-permute-start | bytes 61448 | tf_op jit(solution)/shard_map/while/body/eval_jaxpr/ppermute | solution.py:10
  201.9 11.7 %collective-permute-start.2 = (f32[32,160]{1,0:T(8,128)S(1)}, f32[32,160]{1,0:T(8,128)S(1)}, u32[]{:S(2)}, u32[]{:S(2)}) collective-permute-start(f32[32,160]{1,0:T(8,128)S(1)} %broadcast_select_fusion.2), channel_id=1, source_target_pairs={{0,8},{8,16},{16,24},{24,32},{32,40},{40,48},{48,56},{56,64},{64,7... | collective-permute-start | bytes 61448 | tf_op jit(solution)/shard_map/while/body/eval_jaxpr/ppermute | solution.py:10
  203.8 9.1 %collective-permute-start.1 = (f32[32,160]{1,0:T(8,128)S(1)}, f32[32,160]{1,0:T(8,128)S(1)}, u32[]{:S(2)}, u32[]{:S(2)}) collective-permute-start(f32[32,160]{1,0:T(8,128)S(1)} %get-tuple-element.160), channel_id=1, source_target_pairs={{0,8},{8,16},{16,24},{24,32},{32,40},{40,48},{48,56},{56,64},{64,7... | collective-permute-start | bytes 61448 | tf_op jit(solution)/shard_map/while/body/eval_jaxpr/ppermute | solution.py:10
  216.4 11.7 %collective-permute-start.2 = (f32[32,160]{1,0:T(8,128)S(1)}, f32[32,160]{1,0:T(8,128)S(1)}, u32[]{:S(2)}, u32[]{:S(2)}) collective-permute-start(f32[32,160]{1,0:T(8,128)S(1)} %broadcast_select_fusion.2), channel_id=1, source_target_pairs={{0,8},{8,16},{16,24},{24,32},{32,40},{40,48},{48,56},{56,64},{64,7... | collective-permute-start | bytes 61448 | tf_op jit(solution)/shard_map/while/body/eval_jaxpr/ppermute | solution.py:10
  218.3 9.1 %collective-permute-start.1 = (f32[32,160]{1,0:T(8,128)S(1)}, f32[32,160]{1,0:T(8,128)S(1)}, u32[]{:S(2)}, u32[]{:S(2)}) collective-permute-start(f32[32,160]{1,0:T(8,128)S(1)} %get-tuple-element.160), channel_id=1, source_target_pairs={{0,8},{8,16},{16,24},{24,32},{32,40},{40,48},{48,56},{56,64},{64,7... | collective-permute-start | bytes 61448 | tf_op jit(solution)/shard_map/while/body/eval_jaxpr/ppermute | solution.py:10
  230.9 11.7 %collective-permute-start.2 = (f32[32,160]{1,0:T(8,128)S(1)}, f32[32,160]{1,0:T(8,128)S(1)}, u32[]{:S(2)}, u32[]{:S(2)}) collective-permute-start(f32[32,160]{1,0:T(8,128)S(1)} %broadcast_select_fusion.2), channel_id=1, source_target_pairs={{0,8},{8,16},{16,24},{24,32},{32,40},{40,48},{48,56},{56,64},{64,7... | collective-permute-start | bytes 61448 | tf_op jit(solution)/shard_map/while/body/eval_jaxpr/ppermute | solution.py:10
  232.8 9.1 %collective-permute-start.1 = (f32[32,160]{1,0:T(8,128)S(1)}, f32[32,160]{1,0:T(8,128)S(1)}, u32[]{:S(2)}, u32[]{:S(2)}) collective-permute-start(f32[32,160]{1,0:T(8,128)S(1)} %get-tuple-element.160), channel_id=1, source_target_pairs={{0,8},{8,16},{16,24},{24,32},{32,40},{40,48},{48,56},{56,64},{64,7... | collective-permute-start | bytes 61448 | tf_op jit(solution)/shard_map/while/body/eval_jaxpr/ppermute | solution.py:10
  245.3 11.7 %collective-permute-start.2 = (f32[32,160]{1,0:T(8,128)S(1)}, f32[32,160]{1,0:T(8,128)S(1)}, u32[]{:S(2)}, u32[]{:S(2)}) collective-permute-start(f32[32,160]{1,0:T(8,128)S(1)} %broadcast_select_fusion.2), channel_id=1, source_target_pairs={{0,8},{8,16},{16,24},{24,32},{32,40},{40,48},{48,56},{56,64},{64,7... | collective-permute-start | bytes 61448 | tf_op jit(solution)/shard_map/while/body/eval_jaxpr/ppermute | solution.py:10
  247.3 9.1 %collective-permute-start.1 = (f32[32,160]{1,0:T(8,128)S(1)}, f32[32,160]{1,0:T(8,128)S(1)}, u32[]{:S(2)}, u32[]{:S(2)}) collective-permute-start(f32[32,160]{1,0:T(8,128)S(1)} %get-tuple-element.160), channel_id=1, source_target_pairs={{0,8},{8,16},{16,24},{24,32},{32,40},{40,48},{48,56},{56,64},{64,7... | collective-permute-start | bytes 61448 | tf_op jit(solution)/shard_map/while/body/eval_jaxpr/ppermute | solution.py:10
  259.8 11.7 %collective-permute-start.2 = (f32[32,160]{1,0:T(8,128)S(1)}, f32[32,160]{1,0:T(8,128)S(1)}, u32[]{:S(2)}, u32[]{:S(2)}) collective-permute-start(f32[32,160]{1,0:T(8,128)S(1)} %broadcast_select_fusion.2), channel_id=1, source_target_pairs={{0,8},{8,16},{16,24},{24,32},{32,40},{40,48},{48,56},{56,64},{64,7... | collective-permute-start | bytes 61448 | tf_op jit(solution)/shard_map/while/body/eval_jaxpr/ppermute | solution.py:10
  261.8 9.1 %collective-permute-start.1 = (f32[32,160]{1,0:T(8,128)S(1)}, f32[32,160]{1,0:T(8,128)S(1)}, u32[]{:S(2)}, u32[]{:S(2)}) collective-permute-start(f32[32,160]{1,0:T(8,128)S(1)} %get-tuple-element.160), channel_id=1, source_target_pairs={{0,8},{8,16},{16,24},{24,32},{32,40},{40,48},{48,56},{56,64},{64,7... | collective-permute-start | bytes 61448 | tf_op jit(solution)/shard_map/while/body/eval_jaxpr/ppermute | solution.py:10
  274.3 11.7 %collective-permute-start.2 = (f32[32,160]{1,0:T(8,128)S(1)}, f32[32,160]{1,0:T(8,128)S(1)}, u32[]{:S(2)}, u32[]{:S(2)}) collective-permute-start(f32[32,160]{1,0:T(8,128)S(1)} %broadcast_select_fusion.2), channel_id=1, source_target_pairs={{0,8},{8,16},{16,24},{24,32},{32,40},{40,48},{48,56},{56,64},{64,7... | collective-permute-start | bytes 61448 | tf_op jit(solution)/shard_map/while/body/eval_jaxpr/ppermute | solution.py:10
  276.2 9.1 %collective-permute-start.1 = (f32[32,160]{1,0:T(8,128)S(1)}, f32[32,160]{1,0:T(8,128)S(1)}, u32[]{:S(2)}, u32[]{:S(2)}) collective-permute-start(f32[32,160]{1,0:T(8,128)S(1)} %get-tuple-element.160), channel_id=1, source_target_pairs={{0,8},{8,16},{16,24},{24,32},{32,40},{40,48},{48,56},{56,64},{64,7... | collective-permute-start | bytes 61448 | tf_op jit(solution)/shard_map/while/body/eval_jaxpr/ppermute | solution.py:10
  288.8 11.7 %collective-permute-start.2 = (f32[32,160]{1,0:T(8,128)S(1)}, f32[32,160]{1,0:T(8,128)S(1)}, u32[]{:S(2)}, u32[]{:S(2)}) collective-permute-start(f32[32,160]{1,0:T(8,128)S(1)} %broadcast_select_fusion.2), channel_id=1, source_target_pairs={{0,8},{8,16},{16,24},{24,32},{32,40},{40,48},{48,56},{56,64},{64,7... | collective-permute-start | bytes 61448 | tf_op jit(solution)/shard_map/while/body/eval_jaxpr/ppermute | solution.py:10
  290.7 9.1 %collective-permute-start.1 = (f32[32,160]{1,0:T(8,128)S(1)}, f32[32,160]{1,0:T(8,128)S(1)}, u32[]{:S(2)}, u32[]{:S(2)}) collective-permute-start(f32[32,160]{1,0:T(8,128)S(1)} %get-tuple-element.160), channel_id=1, source_target_pairs={{0,8},{8,16},{16,24},{24,32},{32,40},{40,48},{48,56},{56,64},{64,7... | collective-permute-start | bytes 61448 | tf_op jit(solution)/shard_map/while/body/eval_jaxpr/ppermute | solution.py:10
  303.3 11.7 %collective-permute-start.2 = (f32[32,160]{1,0:T(8,128)S(1)}, f32[32,160]{1,0:T(8,128)S(1)}, u32[]{:S(2)}, u32[]{:S(2)}) collective-permute-start(f32[32,160]{1,0:T(8,128)S(1)} %broadcast_select_fusion.2), channel_id=1, source_target_pairs={{0,8},{8,16},{16,24},{24,32},{32,40},{40,48},{48,56},{56,64},{64,7... | collective-permute-start | bytes 61448 | tf_op jit(solution)/shard_map/while/body/eval_jaxpr/ppermute | solution.py:10
  305.2 9.1 %collective-permute-start.1 = (f32[32,160]{1,0:T(8,128)S(1)}, f32[32,160]{1,0:T(8,128)S(1)}, u32[]{:S(2)}, u32[]{:S(2)}) collective-permute-start(f32[32,160]{1,0:T(8,128)S(1)} %get-tuple-element.160), channel_id=1, source_target_pairs={{0,8},{8,16},{16,24},{24,32},{32,40},{40,48},{48,56},{56,64},{64,7... | collective-permute-start | bytes 61448 | tf_op jit(solution)/shard_map/while/body/eval_jaxpr/ppermute | solution.py:10
  317.8 11.7 %collective-permute-start.2 = (f32[32,160]{1,0:T(8,128)S(1)}, f32[32,160]{1,0:T(8,128)S(1)}, u32[]{:S(2)}, u32[]{:S(2)}) collective-permute-start(f32[32,160]{1,0:T(8,128)S(1)} %broadcast_select_fusion.2), channel_id=1, source_target_pairs={{0,8},{8,16},{16,24},{24,32},{32,40},{40,48},{48,56},{56,64},{64,7... | collective-permute-start | bytes 61448 | tf_op jit(solution)/shard_map/while/body/eval_jaxpr/ppermute | solution.py:10
  319.7 9.1 %collective-permute-start.1 = (f32[32,160]{1,0:T(8,128)S(1)}, f32[32,160]{1,0:T(8,128)S(1)}, u32[]{:S(2)}, u32[]{:S(2)}) collective-permute-start(f32[32,160]{1,0:T(8,128)S(1)} %get-tuple-element.160), channel_id=1, source_target_pairs={{0,8},{8,16},{16,24},{24,32},{32,40},{40,48},{48,56},{56,64},{64,7... | collective-permute-start | bytes 61448 | tf_op jit(solution)/shard_map/while/body/eval_jaxpr/ppermute | solution.py:10
  332.3 11.7 %collective-permute-start.2 = (f32[32,160]{1,0:T(8,128)S(1)}, f32[32,160]{1,0:T(8,128)S(1)}, u32[]{:S(2)}, u32[]{:S(2)}) collective-permute-start(f32[32,160]{1,0:T(8,128)S(1)} %broadcast_select_fusion.2), channel_id=1, source_target_pairs={{0,8},{8,16},{16,24},{24,32},{32,40},{40,48},{48,56},{56,64},{64,7... | collective-permute-start | bytes 61448 | tf_op jit(solution)/shard_map/while/body/eval_jaxpr/ppermute | solution.py:10
  334.2 9.1 %collective-permute-start.1 = (f32[32,160]{1,0:T(8,128)S(1)}, f32[32,160]{1,0:T(8,128)S(1)}, u32[]{:S(2)}, u32[]{:S(2)}) collective-permute-start(f32[32,160]{1,0:T(8,128)S(1)} %get-tuple-element.160), channel_id=1, source_target_pairs={{0,8},{8,16},{16,24},{24,32},{32,40},{40,48},{48,56},{56,64},{64,7... | collective-permute-start | bytes 61448 | tf_op jit(solution)/shard_map/while/body/eval_jaxpr/ppermute | solution.py:10
  346.8 11.7 %collective-permute-start.2 = (f32[32,160]{1,0:T(8,128)S(1)}, f32[32,160]{1,0:T(8,128)S(1)}, u32[]{:S(2)}, u32[]{:S(2)}) collective-permute-start(f32[32,160]{1,0:T(8,128)S(1)} %broadcast_select_fusion.2), channel_id=1, source_target_pairs={{0,8},{8,16},{16,24},{24,32},{32,40},{40,48},{48,56},{56,64},{64,7... | collective-permute-start | bytes 61448 | tf_op jit(solution)/shard_map/while/body/eval_jaxpr/ppermute | solution.py:10
  348.7 9.1 %collective-permute-start.1 = (f32[32,160]{1,0:T(8,128)S(1)}, f32[32,160]{1,0:T(8,128)S(1)}, u32[]{:S(2)}, u32[]{:S(2)}) collective-permute-start(f32[32,160]{1,0:T(8,128)S(1)} %get-tuple-element.160), channel_id=1, source_target_pairs={{0,8},{8,16},{16,24},{24,32},{32,40},{40,48},{48,56},{56,64},{64,7... | collective-permute-start | bytes 61448 | tf_op jit(solution)/shard_map/while/body/eval_jaxpr/ppermute | solution.py:10
  361.2 11.7 %collective-permute-start.2 = (f32[32,160]{1,0:T(8,128)S(1)}, f32[32,160]{1,0:T(8,128)S(1)}, u32[]{:S(2)}, u32[]{:S(2)}) collective-permute-start(f32[32,160]{1,0:T(8,128)S(1)} %broadcast_select_fusion.2), channel_id=1, source_target_pairs={{0,8},{8,16},{16,24},{24,32},{32,40},{40,48},{48,56},{56,64},{64,7... | collective-permute-start | bytes 61448 | tf_op jit(solution)/shard_map/while/body/eval_jaxpr/ppermute | solution.py:10
  363.2 9.1 %collective-permute-start.1 = (f32[32,160]{1,0:T(8,128)S(1)}, f32[32,160]{1,0:T(8,128)S(1)}, u32[]{:S(2)}, u32[]{:S(2)}) collective-permute-start(f32[32,160]{1,0:T(8,128)S(1)} %get-tuple-element.160), channel_id=1, source_target_pairs={{0,8},{8,16},{16,24},{24,32},{32,40},{40,48},{48,56},{56,64},{64,7... | collective-permute-start | bytes 61448 | tf_op jit(solution)/shard_map/while/body/eval_jaxpr/ppermute | solution.py:10
  375.7 11.7 %collective-permute-start.2 = (f32[32,160]{1,0:T(8,128)S(1)}, f32[32,160]{1,0:T(8,128)S(1)}, u32[]{:S(2)}, u32[]{:S(2)}) collective-permute-start(f32[32,160]{1,0:T(8,128)S(1)} %broadcast_select_fusion.2), channel_id=1, source_target_pairs={{0,8},{8,16},{16,24},{24,32},{32,40},{40,48},{48,56},{56,64},{64,7... | collective-permute-start | bytes 61448 | tf_op jit(solution)/shard_map/while/body/eval_jaxpr/ppermute | solution.py:10
  377.7 9.1 %collective-permute-start.1 = (f32[32,160]{1,0:T(8,128)S(1)}, f32[32,160]{1,0:T(8,128)S(1)}, u32[]{:S(2)}, u32[]{:S(2)}) collective-permute-start(f32[32,160]{1,0:T(8,128)S(1)} %get-tuple-element.160), channel_id=1, source_target_pairs={{0,8},{8,16},{16,24},{24,32},{32,40},{40,48},{48,56},{56,64},{64,7... | collective-permute-start | bytes 61448 | tf_op jit(solution)/shard_map/while/body/eval_jaxpr/ppermute | solution.py:10
  390.2 11.7 %collective-permute-start.2 = (f32[32,160]{1,0:T(8,128)S(1)}, f32[32,160]{1,0:T(8,128)S(1)}, u32[]{:S(2)}, u32[]{:S(2)}) collective-permute-start(f32[32,160]{1,0:T(8,128)S(1)} %broadcast_select_fusion.2), channel_id=1, source_target_pairs={{0,8},{8,16},{16,24},{24,32},{32,40},{40,48},{48,56},{56,64},{64,7... | collective-permute-start | bytes 61448 | tf_op jit(solution)/shard_map/while/body/eval_jaxpr/ppermute | solution.py:10
  392.1 9.1 %collective-permute-start.1 = (f32[32,160]{1,0:T(8,128)S(1)}, f32[32,160]{1,0:T(8,128)S(1)}, u32[]{:S(2)}, u32[]{:S(2)}) collective-permute-start(f32[32,160]{1,0:T(8,128)S(1)} %get-tuple-element.160), channel_id=1, source_target_pairs={{0,8},{8,16},{16,24},{24,32},{32,40},{40,48},{48,56},{56,64},{64,7... | collective-permute-start | bytes 61448 | tf_op jit(solution)/shard_map/while/body/eval_jaxpr/ppermute | solution.py:10
  404.7 11.7 %collective-permute-start.2 = (f32[32,160]{1,0:T(8,128)S(1)}, f32[32,160]{1,0:T(8,128)S(1)}, u32[]{:S(2)}, u32[]{:S(2)}) collective-permute-start(f32[32,160]{1,0:T(8,128)S(1)} %broadcast_select_fusion.2), channel_id=1, source_target_pairs={{0,8},{8,16},{16,24},{24,32},{32,40},{40,48},{48,56},{56,64},{64,7... | collective-permute-start | bytes 61448 | tf_op jit(solution)/shard_map/while/body/eval_jaxpr/ppermute | solution.py:10
  406.6 9.1 %collective-permute-start.1 = (f32[32,160]{1,0:T(8,128)S(1)}, f32[32,160]{1,0:T(8,128)S(1)}, u32[]{:S(2)}, u32[]{:S(2)}) collective-permute-start(f32[32,160]{1,0:T(8,128)S(1)} %get-tuple-element.160), channel_id=1, source_target_pairs={{0,8},{8,16},{16,24},{24,32},{32,40},{40,48},{48,56},{56,64},{64,7... | collective-permute-start | bytes 61448 | tf_op jit(solution)/shard_map/while/body/eval_jaxpr/ppermute | solution.py:10
  419.2 11.7 %collective-permute-start.2 = (f32[32,160]{1,0:T(8,128)S(1)}, f32[32,160]{1,0:T(8,128)S(1)}, u32[]{:S(2)}, u32[]{:S(2)}) collective-permute-start(f32[32,160]{1,0:T(8,128)S(1)} %broadcast_select_fusion.2), channel_id=1, source_target_pairs={{0,8},{8,16},{16,24},{24,32},{32,40},{40,48},{48,56},{56,64},{64,7... | collective-permute-start | bytes 61448 | tf_op jit(solution)/shard_map/while/body/eval_jaxpr/ppermute | solution.py:10
  421.1 9.1 %collective-permute-start.1 = (f32[32,160]{1,0:T(8,128)S(1)}, f32[32,160]{1,0:T(8,128)S(1)}, u32[]{:S(2)}, u32[]{:S(2)}) collective-permute-start(f32[32,160]{1,0:T(8,128)S(1)} %get-tuple-element.160), channel_id=1, source_target_pairs={{0,8},{8,16},{16,24},{24,32},{32,40},{40,48},{48,56},{56,64},{64,7... | collective-permute-start | bytes 61448 | tf_op jit(solution)/shard_map/while/body/eval_jaxpr/ppermute | solution.py:10
  433.7 11.7 %collective-permute-start.2 = (f32[32,160]{1,0:T(8,128)S(1)}, f32[32,160]{1,0:T(8,128)S(1)}, u32[]{:S(2)}, u32[]{:S(2)}) collective-permute-start(f32[32,160]{1,0:T(8,128)S(1)} %broadcast_select_fusion.2), channel_id=1, source_target_pairs={{0,8},{8,16},{16,24},{24,32},{32,40},{40,48},{48,56},{56,64},{64,7... | collective-permute-start | bytes 61448 | tf_op jit(solution)/shard_map/while/body/eval_jaxpr/ppermute | solution.py:10
  435.6 9.1 %collective-permute-start.1 = (f32[32,160]{1,0:T(8,128)S(1)}, f32[32,160]{1,0:T(8,128)S(1)}, u32[]{:S(2)}, u32[]{:S(2)}) collective-permute-start(f32[32,160]{1,0:T(8,128)S(1)} %get-tuple-element.160), channel_id=1, source_target_pairs={{0,8},{8,16},{16,24},{24,32},{32,40},{40,48},{48,56},{56,64},{64,7... | collective-permute-start | bytes 61448 | tf_op jit(solution)/shard_map/while/body/eval_jaxpr/ppermute | solution.py:10
  448.2 11.7 %collective-permute-start.2 = (f32[32,160]{1,0:T(8,128)S(1)}, f32[32,160]{1,0:T(8,128)S(1)}, u32[]{:S(2)}, u32[]{:S(2)}) collective-permute-start(f32[32,160]{1,0:T(8,128)S(1)} %broadcast_select_fusion.2), channel_id=1, source_target_pairs={{0,8},{8,16},{16,24},{24,32},{32,40},{40,48},{48,56},{56,64},{64,7... | collective-permute-start | bytes 61448 | tf_op jit(solution)/shard_map/while/body/eval_jaxpr/ppermute | solution.py:10
  450.1 9.1 %collective-permute-start.1 = (f32[32,160]{1,0:T(8,128)S(1)}, f32[32,160]{1,0:T(8,128)S(1)}, u32[]{:S(2)}, u32[]{:S(2)}) collective-permute-start(f32[32,160]{1,0:T(8,128)S(1)} %get-tuple-element.160), channel_id=1, source_target_pairs={{0,8},{8,16},{16,24},{24,32},{32,40},{40,48},{48,56},{56,64},{64,7... | collective-permute-start | bytes 61448 | tf_op jit(solution)/shard_map/while/body/eval_jaxpr/ppermute | solution.py:10
  462.7 11.7 %collective-permute-start.2 = (f32[32,160]{1,0:T(8,128)S(1)}, f32[32,160]{1,0:T(8,128)S(1)}, u32[]{:S(2)}, u32[]{:S(2)}) collective-permute-start(f32[32,160]{1,0:T(8,128)S(1)} %broadcast_select_fusion.2), channel_id=1, source_target_pairs={{0,8},{8,16},{16,24},{24,32},{32,40},{40,48},{48,56},{56,64},{64,7... | collective-permute-start | bytes 61448 | tf_op jit(solution)/shard_map/while/body/eval_jaxpr/ppermute | solution.py:10
  464.6 9.1 %collective-permute-start.1 = (f32[32,160]{1,0:T(8,128)S(1)}, f32[32,160]{1,0:T(8,128)S(1)}, u32[]{:S(2)}, u32[]{:S(2)}) collective-permute-start(f32[32,160]{1,0:T(8,128)S(1)} %get-tuple-element.160), channel_id=1, source_target_pairs={{0,8},{8,16},{16,24},{24,32},{32,40},{40,48},{48,56},{56,64},{64,7... | collective-permute-start | bytes 61448 | tf_op jit(solution)/shard_map/while/body/eval_jaxpr/ppermute | solution.py:10
  477.1 11.7 %collective-permute-start.2 = (f32[32,160]{1,0:T(8,128)S(1)}, f32[32,160]{1,0:T(8,128)S(1)}, u32[]{:S(2)}, u32[]{:S(2)}) collective-permute-start(f32[32,160]{1,0:T(8,128)S(1)} %broadcast_select_fusion.2), channel_id=1, source_target_pairs={{0,8},{8,16},{16,24},{24,32},{32,40},{40,48},{48,56},{56,64},{64,7... | collective-permute-start | bytes 61448 | tf_op jit(solution)/shard_map/while/body/eval_jaxpr/ppermute | solution.py:10
  479.1 9.1 %collective-permute-start.1 = (f32[32,160]{1,0:T(8,128)S(1)}, f32[32,160]{1,0:T(8,128)S(1)}, u32[]{:S(2)}, u32[]{:S(2)}) collective-permute-start(f32[32,160]{1,0:T(8,128)S(1)} %get-tuple-element.160), channel_id=1, source_target_pairs={{0,8},{8,16},{16,24},{24,32},{32,40},{40,48},{48,56},{56,64},{64,7... | collective-permute-start | bytes 61448 | tf_op jit(solution)/shard_map/while/body/eval_jaxpr/ppermute | solution.py:10
  491.6 11.7 %collective-permute-start.2 = (f32[32,160]{1,0:T(8,128)S(1)}, f32[32,160]{1,0:T(8,128)S(1)}, u32[]{:S(2)}, u32[]{:S(2)}) collective-permute-start(f32[32,160]{1,0:T(8,128)S(1)} %broadcast_select_fusion.2), channel_id=1, source_target_pairs={{0,8},{8,16},{16,24},{24,32},{32,40},{40,48},{48,56},{56,64},{64,7... | collective-permute-start | bytes 61448 | tf_op jit(solution)/shard_map/while/body/eval_jaxpr/ppermute | solution.py:10
  493.6 9.1 %collective-permute-start.1 = (f32[32,160]{1,0:T(8,128)S(1)}, f32[32,160]{1,0:T(8,128)S(1)}, u32[]{:S(2)}, u32[]{:S(2)}) collective-permute-start(f32[32,160]{1,0:T(8,128)S(1)} %get-tuple-element.160), channel_id=1, source_target_pairs={{0,8},{8,16},{16,24},{24,32},{32,40},{40,48},{48,56},{56,64},{64,7... | collective-permute-start | bytes 61448 | tf_op jit(solution)/shard_map/while/body/eval_jaxpr/ppermute | solution.py:10
  506.1 11.7 %collective-permute-start.2 = (f32[32,160]{1,0:T(8,128)S(1)}, f32[32,160]{1,0:T(8,128)S(1)}, u32[]{:S(2)}, u32[]{:S(2)}) collective-permute-start(f32[32,160]{1,0:T(8,128)S(1)} %broadcast_select_fusion.2), channel_id=1, source_target_pairs={{0,8},{8,16},{16,24},{24,32},{32,40},{40,48},{48,56},{56,64},{64,7... | collective-permute-start | bytes 61448 | tf_op jit(solution)/shard_map/while/body/eval_jaxpr/ppermute | solution.py:10
  508.1 9.1 %collective-permute-start.1 = (f32[32,160]{1,0:T(8,128)S(1)}, f32[32,160]{1,0:T(8,128)S(1)}, u32[]{:S(2)}, u32[]{:S(2)}) collective-permute-start(f32[32,160]{1,0:T(8,128)S(1)} %get-tuple-element.160), channel_id=1, source_target_pairs={{0,8},{8,16},{16,24},{24,32},{32,40},{40,48},{48,56},{56,64},{64,7... | collective-permute-start | bytes 61448 | tf_op jit(solution)/shard_map/while/body/eval_jaxpr/ppermute | solution.py:10
  520.6 11.7 %collective-permute-start.2 = (f32[32,160]{1,0:T(8,128)S(1)}, f32[32,160]{1,0:T(8,128)S(1)}, u32[]{:S(2)}, u32[]{:S(2)}) collective-permute-start(f32[32,160]{1,0:T(8,128)S(1)} %broadcast_select_fusion.2), channel_id=1, source_target_pairs={{0,8},{8,16},{16,24},{24,32},{32,40},{40,48},{48,56},{56,64},{64,7... | collective-permute-start | bytes 61448 | tf_op jit(solution)/shard_map/while/body/eval_jaxpr/ppermute | solution.py:10
  522.5 9.1 %collective-permute-start.1 = (f32[32,160]{1,0:T(8,128)S(1)}, f32[32,160]{1,0:T(8,128)S(1)}, u32[]{:S(2)}, u32[]{:S(2)}) collective-permute-start(f32[32,160]{1,0:T(8,128)S(1)} %get-tuple-element.160), channel_id=1, source_target_pairs={{0,8},{8,16},{16,24},{24,32},{32,40},{40,48},{48,56},{56,64},{64,7... | collective-permute-start | bytes 61448 | tf_op jit(solution)/shard_map/while/body/eval_jaxpr/ppermute | solution.py:10
  535.1 11.7 %collective-permute-start.2 = (f32[32,160]{1,0:T(8,128)S(1)}, f32[32,160]{1,0:T(8,128)S(1)}, u32[]{:S(2)}, u32[]{:S(2)}) collective-permute-start(f32[32,160]{1,0:T(8,128)S(1)} %broadcast_select_fusion.2), channel_id=1, source_target_pairs={{0,8},{8,16},{16,24},{24,32},{32,40},{40,48},{48,56},{56,64},{64,7... | collective-permute-start | bytes 61448 | tf_op jit(solution)/shard_map/while/body/eval_jaxpr/ppermute | solution.py:10
  537.0 9.1 %collective-permute-start.1 = (f32[32,160]{1,0:T(8,128)S(1)}, f32[32,160]{1,0:T(8,128)S(1)}, u32[]{:S(2)}, u32[]{:S(2)}) collective-permute-start(f32[32,160]{1,0:T(8,128)S(1)} %get-tuple-element.160), channel_id=1, source_target_pairs={{0,8},{8,16},{16,24},{24,32},{32,40},{40,48},{48,56},{56,64},{64,7... | collective-permute-start | bytes 61448 | tf_op jit(solution)/shard_map/while/body/eval_jaxpr/ppermute | solution.py:10
  549.6 9.1 %collective-permute-start.3 = (f32[32,160]{1,0:T(8,128)S(1)}, f32[32,160]{1,0:T(8,128)S(1)}, u32[]{:S(2)}, u32[]{:S(2)}) collective-permute-start(f32[32,160]{1,0:T(8,128)S(1)} %get-tuple-element.51), channel_id=1, source_target_pairs={{0,8},{8,16},{16,24},{24,32},{32,40},{40,48},{48,56},{56,64},{64,7... | collective-permute-start | bytes 61448 | tf_op jit(solution)/shard_map/ppermute | solution.py:10
  561.0 95.3 %collective-permute-start.5 = (f32[32,160]{1,0:T(8,128)S(1)}, f32[32,160]{1,0:T(8,128)S(1)}, u32[]{:S(2)}, u32[]{:S(2)}) collective-permute-start(f32[32,160]{1,0:T(8,128)S(1)} %get-tuple-element.53), channel_id=1, source_target_pairs={{0,264},{8,272},{16,280},{24,288},{32,296},{40,304},{48,312},{56,3... | collective-permute-start | bytes 61448 | tf_op jit(solution)/shard_map/ppermute | solution.py:10
  (35 other events, 299.6 us)
Sparse Core Ops, SparseCore 0:
  561.1 94.2 reduce-scatter.3
where the time goes:
time: 668 us; the launch traced here: 664 us
  waiting for transfers between devices  274 us (41%)
  starting transfers between devices  204 us (31%)
  matrix products  86.6 us (13%)
  blocking collectives  76.8 us (11%)
  between operations  13.5 us (2%)
    ppermute x96, starting transfers between devices, shifted(): return lax.ppermute(value, axis, pairs)  204 us
    ppermute x96, waiting for transfers between devices, shifted(): return lax.ppermute(value, axis, pairs)  183 us
    unnamed x2, waiting for transfers between devices  91.5 us
    dot_general x33, matrix products, matern_tile(): lax.dot_general(col_z, row_z, (((0,), (0,)), ((), ())), precision=lax.Pre...  40.7 us
    all_gather x1, blocking collectives, per_device(): lax.all_gather(local_z, 'rep', axis=1, tiled=True)  39.1 us
    all_gather x1, blocking collectives, per_device(): lax.all_gather(vectors, 'rep', axis=1, tiled=True)  37.7 us
    dot_general x31, matrix products, cols_times(): lax.dot_general(row_v, kernel, (((1,), (1,)), ((), ())), precision=lax.Pr...  26.3 us
    dot_general x33, matrix products, rows_times(): lax.dot(col_v, kernel, precision=lax.Precision.HIGHEST, preferred_element...  19.6 us
  transfers between devices with their start and end apart: 97, of which 64 were waited for; matrix products, arithmetic and copies ran while one was open for 9% of the time, Pallas kernels for 0%

commit v1 on v0

v1 whole, which is shorter than its diff:
```python
import functools
import math
import jax
import jax.numpy as jnp
from jax import lax
from jax.experimental import pallas as pl
from jax.experimental.pallas import tpu as pltpu
from jax.sharding import PartitionSpec as P

F = jnp.float32
H = jnp.bfloat16
LN2 = math.log(2.0)
ALPHA = 1.5 / LN2
BETA = 0.75 / (LN2 * LN2)
SCALE = math.sqrt(5.0) / LN2
GAIN = (LN2 * LN2 / 3.0) * 2.0**ALPHA
TINY = 1e-30
TJ, TI = 256, 512

SYM = [(0, 1), (1, 0), (0, 2), (1, 1), (-1, 1), (0, 3), (1, 2), (-1, 2), (1, 3), (-1, 3), (2, 1), (2, 2), (2, 3), (-1, 4)]
OWN = [(0, 0), (2, 0), (0, 4), (2, 4)]
COLS = SYM + OWN
NROW, NCOL, NSYM = 16, len(COLS), len(SYM)
CHUNK_I = NROW + NROW // 4
CHUNK_S = NSYM + -(-NSYM // 4)
CHUNK_O = len(OWN) + -(-len(OWN) // 4) + 1
NI, NJ = CHUNK_I * 128, (CHUNK_S + CHUNK_O) * 128


def split3(value):
    first = value.astype(H).astype(F)
    rest = value - first
    second = rest.astype(H).astype(F)
    return first, second, rest - second


def stacked(*rows):
    index = lax.broadcasted_iota(jnp.int32, (16, 128), 0)
    out = jnp.zeros((16, 128), F)
    for k, value in enumerate(rows):
        out = jnp.where(index == k, value, out)
    return out


def pieces(z, row_side):
    square = jnp.sum(z * z, axis=0, keepdims=True)
    n1, n2, n3 = split3(square)
    x1, x2, x3 = split3(z)
    one, zero = jnp.ones_like(square), jnp.zeros((16, 128), F)
    if row_side:
        parts = [x1, x2, x1, x2, x3, x1, stacked(n1, n2, n3, one, one, one), zero]
    else:
        x1, x2, x3 = -2.0 * x1, -2.0 * x2, -2.0 * x3
        parts = [x1, x1, x2, x2, x1, x3, stacked(one, one, one, n1, n2, n3), zero]
    return jnp.concatenate(parts, axis=0)


def lanes(chunk):
    if isinstance(chunk, int):
        return pl.ds(128 * chunk, 128)
    return pl.ds(pl.multiple_of(chunk * 128, 128), 128)


def put(chunk, z, v, row_side, pts, vec):
    wide = pieces(z, row_side)
    if row_side:
        pts[:, lanes(chunk)] = wide.astype(H)
    else:
        pts[lanes(chunk), :] = wide.T.astype(H)
    high = v.astype(H)
    vec[0:32, lanes(chunk)] = high
    vec[32:64, lanes(chunk)] = (v - high.astype(F)).astype(H)


def prepare(src, first, count, chunk0, row_side, pts, vec):
    @pl.loop(0, count)
    def _(s):
        put(s + chunk0, src[first + s, 0:16, :], src[first + s, 16:48, :], row_side, pts, vec)

    group_of = lax.broadcasted_iota(jnp.int32, (16, 128), 1) // 32
    for g in range(-(-count // 4)):
        outs = [jnp.zeros((16, 128), F) for _ in range(3)]
        for k in range(min(4, count - 4 * g)):
            rem = src[first + 4 * g + k, 48:64, :]
            for q in range(3):
                turn = (32 * (k - q)) % 128
                outs[q] = jnp.where(group_of == k, pltpu.roll(rem, turn, 1) if turn else rem, outs[q])
        put(chunk0 + count + g, outs[0], jnp.concatenate(outs[1:], axis=0), row_side, pts, vec)


def finish(acc, chunk0, count, out, first):
    group_of = lax.broadcasted_iota(jnp.int32, (8, 128), 1) // 32
    for s in range(count):
        c = lanes(chunk0 + s)
        out[first + s, 0:32, :] = (acc[0:32, c] + acc[32:64, c]) * GAIN
    for g in range(-(-count // 4)):
        c = lanes(chunk0 + count + g)
        t = (acc[0:32, c] + acc[32:64, c]) * GAIN
        for k in range(min(4, count - 4 * g)):
            o = jnp.zeros((8, 128), F)
            for q in range(4):
                turn = (32 * (q - k)) % 128
                piece = t[8 * q : 8 * q + 8, :]
                o = jnp.where(group_of == q, pltpu.roll(piece, turn, 1) if turn else piece, o)
            out[first + 4 * g + k, 32:40, :] = o


def products(A, vj, B, vi, acc_i, acc_j, d0, d1, k0, k1):
    nit = NI // TI
    total = nit * (NJ // TJ)

    def place(t):
        return (
            pl.ds(pl.multiple_of(lax.div(t, nit) * TJ, TJ), TJ),
            pl.ds(pl.multiple_of(lax.rem(t, nit) * TI, TI), TI),
        )

    def distances(t, d):
        sj, si = place(t)
        d[...] = jnp.dot(A[sj, :], B[:, si], preferred_element_type=F)

    def kernel_values(d, k):
        x = jnp.maximum(d[...], TINY)
        u = (-ALPHA) - x * lax.rsqrt(x)
        value = (u * u + BETA) * jnp.exp2(u)
        high = value.astype(H)
        k[0] = high
        k[1] = (value - high.astype(F)).astype(H)

    def accumulate(t, k):
        sj, si = place(t)
        v_j, v_i = vj[:, sj], vi[:, si]
        acc_i[:, si] += jnp.dot(
            jnp.concatenate([v_j, v_j], axis=1), jnp.concatenate([k[0], k[1]], axis=0), preferred_element_type=F
        )
        acc_j[:, sj] += lax.dot_general(
            jnp.concatenate([v_i, v_i], axis=1),
            jnp.concatenate([k[0], k[1]], axis=1),
            (((1,), (1,)), ((), ())),
            preferred_element_type=F,
        )

    distances(0, d0)

    @pl.loop(0, total // 2)
    def _(m):
        a = 2 * m
        accumulate(jnp.maximum(a - 1, 0), k1)
        distances(a + 1, d1)
        kernel_values(d0, k0)
        accumulate(a, k0)
        distances(jnp.minimum(a + 2, total - 1), d0)
        kernel_values(d1, k1)

    accumulate(total - 1, k1)


def solve_kernel(p_ref, v_ref, l_ref, out_ref, R, C, B, vi, A, vj, acc_i, acc_j, d0, d1, k0, k1, oi, oj, gi, gj,
                 rs, rr, cs, cr, ris, rir, cjs, cjr):
    b, r = lax.axis_index("blk"), lax.axis_index("rep")
    core, z, x = lax.rem(b, 2), lax.div(b, 8), lax.rem(r, 4)
    y = lax.div(r, 4) * 4 + lax.rem(lax.div(b, 2), 4)

    def at(dx=0, dy=0, dz=0, dc=0):
        xx, yy, zz = lax.rem(x + dx + 4, 4), lax.rem(y + dy + 8, 8), lax.rem(z + dz + 8, 8)
        cc = 1 - core if dc else core
        return ((zz * 4 + lax.rem(yy, 4)) * 2 + cc, lax.div(yy, 4) * 4 + xx)

    own = R.at[0]
    scaled = p_ref[...] / l_ref[...] * SCALE
    R[0, 0:16, :] = scaled[:, 0:128]
    R[0, 16:48, :] = v_ref[:, 0:128]
    R[0, 48:64, 0:32] = scaled[:, 128:160]
    R[0, 48:64, 32:64] = v_ref[0:16, 128:160]
    R[0, 48:64, 64:96] = v_ref[16:32, 128:160]
    R[0, 48:64, 96:128] = jnp.zeros((16, 32), F)
    C[NSYM] = R[0]

    barrier = pltpu.get_barrier_semaphore()
    near = [at(dc=1), at(dz=1), at(dz=-1), at(dy=1), at(dy=-1), at(dx=1), at(dx=-1)]
    for d in near:
        pl.semaphore_signal(barrier, inc=1, device_id=d, device_id_type=pl.DeviceIdType.MESH)
    pl.semaphore_wait(barrier, len(near))

    def send(source, dest, ss, rsem, where):
        return pltpu.make_async_remote_copy(
            src_ref=source, dst_ref=dest, send_sem=ss, recv_sem=rsem, device_id=where,
            device_id_type=pl.DeviceIdType.MESH,
        )

    row, col = {}, {}
    for dz in range(8):
        for dc in range(2):
            s = 2 * dz + dc
            if s == 0:
                continue
            if dc:
                source, where = R.at[2 * dz], at(dc=1)
            elif dz <= 4:
                source, where = R.at[2 * (dz - 1)], at(dz=-1)
            else:
                source, where = R.at[2 * ((dz + 1) % 8)], at(dz=1)
            row[dz, dc] = send(source, R.at[s], rs.at[s], rr.at[s], where)
    slot = {o: k for k, o in enumerate(COLS)}
    for (dx, dy), s in slot.items():
        if (dx, dy) == (0, 0):
            continue
        if dx == 0:
            prev, where = (0, dy - 1), at(dy=-1)
        elif dx == 1:
            prev, where = (0, dy), at(dx=-1)
        elif dx == -1:
            prev, where = (0, dy), at(dx=1)
        elif dy <= 1:
            prev, where = (1, dy), at(dx=-1)
        else:
            prev, where = (-1, dy), at(dx=1)
        source = own if prev == (0, 0) else C.at[slot[prev]]
        col[dx, dy] = send(source, C.at[s], cs.at[s], cr.at[s], where)

    for t in (col[0, 1], row[1, 0], row[7, 0], col[1, 0], row[0, 1]):
        t.start()
    got_row, got_col = [], []

    def arrive_row(dz, *then):
        row[dz, 0].wait_recv()
        for t in then:
            row[t, 0].start()
        row[dz, 1].start()

    def arrive_col(o, *then):
        col[o].wait_recv()
        for t in then:
            col[t].start()

    arrive_col((0, 1), (0, 2), (1, 1), (-1, 1))
    arrive_row(1, 2)
    arrive_row(7, 6)
    arrive_col((1, 0), (2, 0))
    arrive_col((0, 2), (0, 3), (1, 2), (-1, 2))
    arrive_row(2, 3)
    arrive_row(6, 5)
    arrive_col((1, 1), (2, 1))
    arrive_col((0, 3), (0, 4), (1, 3), (-1, 3))
    arrive_row(3, 4)
    arrive_row(5)
    arrive_col((-1, 2), (2, 2))
    arrive_col((0, 4), (-1, 4))
    arrive_row(4)
    arrive_col((-1, 3), (2, 3))
    arrive_col((-1, 4), (2, 4))
    for o in ((-1, 1), (1, 2), (1, 3), (2, 0), (2, 1), (2, 2), (2, 3), (2, 4)):
        arrive_col(o)
    for dz in range(8):
        row[dz, 1].wait_recv()

    prepare(R, 0, NROW, 0, True, B, vi)
    prepare(C, 0, NSYM, 0, False, A, vj)
    prepare(C, NSYM, len(OWN), CHUNK_S, False, A, vj)
    pad = pl.ds(NJ - 128, 128)
    A[pad, :] = jnp.zeros((128, 128), H)
    vj[:, pad] = jnp.zeros((64, 128), H)
    acc_i[...] = jnp.zeros_like(acc_i)
    acc_j[...] = jnp.zeros_like(acc_j)
    k1[...] = jnp.zeros_like(k1)
    products(A, vj, B, vi, acc_i, acc_j, d0, d1, k0, k1)

    finish(acc_j, 0, NSYM, oj, 0)
    backs = []
    for k, (dx, dy) in enumerate(SYM):
        t = send(oj.at[k], gj.at[k], cjs.at[k], cjr.at[k], at(dx=dx, dy=dy))
        t.start()
        backs.append(t)
    finish(acc_i, 0, NROW, oi, 0)
    for dz in (4, 3, 5, 2, 6, 1, 7, 0):
        for dc in (0, 1):
            if dz == 0 and dc == 0:
                continue
            s, d = 2 * dz + dc, 2 * ((8 - dz) % 8) + dc
            t = send(oi.at[s], gi.at[d], ris.at[d], rir.at[d], at(dz=dz, dc=dc))
            t.start()
            backs.append(t)
    total = oi[0]
    for t in backs:
        t.wait_recv()
    for s in range(1, NROW):
        total = total + gi[s]
    for k in range(NSYM):
        total = total + gj[k]
    out_ref[:, 0:128] = total[0:32]
    rem = total[32:40]
    for q in range(4):
        turned = pltpu.roll(rem, (-32 * q) % 128, 1) if q else rem
        out_ref[8 * q : 8 * q + 8, 128:160] = turned[:, 0:32]
    for t in (*row.values(), *col.values(), *backs):
        t.wait_send()


def per_device(points, vectors, lengthscales):
    vmem = pl.BlockSpec(memory_space=pltpu.VMEM)
    dma = pltpu.SemaphoreType.DMA
    return pl.pallas_call(
        solve_kernel,
        out_shape=jax.ShapeDtypeStruct(vectors.shape, F),
        in_specs=[vmem] * 3,
        out_specs=vmem,
        scratch_shapes=[
            pltpu.VMEM((NROW, 64, 128), F),
            pltpu.VMEM((NCOL, 64, 128), F),
            pltpu.VMEM((128, NI), H),
            pltpu.VMEM((64, NI), H),
            pltpu.VMEM((NJ, 128), H),
            pltpu.VMEM((64, NJ), H),
            pltpu.VMEM((64, NI), F),
            pltpu.VMEM((64, NJ), F),
            pltpu.VMEM((TJ, TI), F),
            pltpu.VMEM((TJ, TI), F),
            pltpu.VMEM((2, TJ, TI), H),
            pltpu.VMEM((2, TJ, TI), H),
            pltpu.VMEM((NROW, 40, 128), F),
            pltpu.VMEM((NSYM, 40, 128), F),
            pltpu.VMEM((NROW, 40, 128), F),
            pltpu.VMEM((NSYM, 40, 128), F),
            dma((NROW,)), dma((NROW,)), dma((NCOL,)), dma((NCOL,)),
            dma((NROW,)), dma((NROW,)), dma((NSYM,)), dma((NSYM,)),
        ],
        compiler_params=pltpu.CompilerParams(collective_id=0, has_side_effects=True),
        name="solve",
    )(points, vectors, lengthscales[:, None])


def solution(mesh):
    return jax.shard_map(
        per_device,
        mesh=mesh,
        in_specs=(P(None, ("blk", "rep")), P(None, ("blk", "rep")), P()),
        out_specs=P(None, ("blk", "rep")),
        check_vma=False,
    )
```

time: 668 us -> 74.5 us (0.11)
  waiting for transfers between devices: 274 us -> 0 us
  starting transfers between devices: 204 us -> 0 us
  matrix products: 86.6 us -> 0 us
  blocking collectives: 76.8 us -> 0 us
  Pallas kernels: 0 us -> 70.4 us
  between operations: 13.5 us -> 0.01 us
    ppermute x96 -> x0, starting transfers between devices: 204 us -> none  [shifted(): return lax.ppermute(value, axis, pairs)]
    ppermute x96 -> x0, waiting for transfers between devices: 183 us -> none  [shifted(): return lax.ppermute(value, axis, pairs)]
    unnamed x2 -> x0, waiting for transfers between devices: 91.5 us -> none
    dot_general x97 -> x0, matrix products: 86.6 us -> none  [the longest x33 40.7 us: matern_tile(): lax.dot_general(col_z, row_z, (((0,), (0,)), ((), ())), precision=lax.Pre...]
    all_gather x2 -> x0, blocking collectives: 76.8 us -> none  [the longest x1 39.1 us: per_device(): lax.all_gather(local_z, 'rep', axis=1, tiled=True)]
    pallas_call x0 -> x1, Pallas kernels: none -> 70.4 us  [per_device(): pl.pallas_call(solve_kernel, out_shape=jax.ShapeDtypeStruct(vectors.shape...]
  transfers between devices with their start and end apart: 97 -> 0, of which waited for: 64 -> 0; matrix products, arithmetic and copies ran while one was open for 9% -> 0% of each run, Pallas kernels for 0% -> 0%
where the time goes in v1:
time: 74.5 us; the launch traced here: 73.1 us
  Pallas kernels  70.4 us (94%)
  local copies, waits for them, and re-layouts  2.71 us (4%)
    pallas_call x1, Pallas kernels, per_device(): pl.pallas_call(solve_kernel, out_shape=jax.ShapeDtypeStruct(vectors.shape...  70.4 us
    unnamed x3, local copies, waits for them, and re-layouts  2.03 us

profile of v1, /device:TPU:1, one launch (start us, length us, event | category | flops | bytes accessed | tf_op | source)
XLA Modules:
  0.0 73.1 jit_solution(16108798795424986577)
XLA Ops:
  0.0 0.0 copy-start
  0.0 0.7 copy-done
  0.7 0.7 copy.4.l_ref
  1.3 70.4 %solve.1 = f32[32,160]{1,0:T(8,128)} custom-call(f32[16,160]{1,0:T(8,128)} %p_ref.1, f32[32,160]{1,0:T(8,128)} %v_ref.1, f32[16,1]{1,0:T(8,128)} %copy.4.l_ref), custom_call_target="tpu_custom_call" | custom-call | tf_op jit(solution)/shard_map/solve/pallas_call | solution.py:302
  71.8 1.4 %copy.6 = f32[32,160]{1,0:T(8,128)} copy(f32[32,160]{1,0:T(8,128)} %solve.1) | data formatting | bytes 40960
Async XLA Ops:
  0.0 0.7 copy-start

commit v2 on v1

v2 whole, which is shorter than its diff:
```python
import functools
import math
import jax
import jax.numpy as jnp
from jax import lax
from jax.experimental import pallas as pl
from jax.experimental.pallas import tpu as pltpu
from jax.sharding import PartitionSpec as P

F = jnp.float32
H = jnp.bfloat16
LN2 = math.log(2.0)
ALPHA = 1.5 / LN2
BETA = 0.75 / (LN2 * LN2)
SCALE = math.sqrt(5.0) / LN2
GAIN = (LN2 * LN2 / 3.0) * 2.0**ALPHA
TINY = 1e-30
TILE = 256

ROWS = [0, 1, 7, 2, 6, 3, 5, 4]
SYM = [(0, 1), (1, 0), (0, 2), (1, 1), (-1, 1), (0, 3), (1, 2), (-1, 2), (2, 1), (1, 3), (-1, 3), (2, 2), (2, 3), (-1, 4)]
OWN = [(0, 0), (2, 0), (0, 4), (2, 4)]
COLS = SYM + OWN
NROW, NCOL, NSYM = 16, len(COLS), len(SYM)
CHUNK_S = NSYM + -(-NSYM // 4)
NI, NJ = 128 * (NROW + NROW // 4), 128 * 24


def split3(value):
    first = value.astype(H).astype(F)
    rest = value - first
    second = rest.astype(H).astype(F)
    return first, second, rest - second


def stacked(*rows):
    index = lax.broadcasted_iota(jnp.int32, (16, 128), 0)
    out = jnp.zeros((16, 128), F)
    for k, value in enumerate(rows):
        out = jnp.where(index == k, value, out)
    return out


def pieces(z, row_side):
    square = jnp.sum(z * z, axis=0, keepdims=True)
    n1, n2, n3 = split3(square)
    x1, x2, x3 = split3(z)
    one, zero = jnp.ones_like(square), jnp.zeros((16, 128), F)
    if row_side:
        parts = [x1, x2, x1, x2, x3, x1, stacked(n1, n2, n3, one, one, one), zero]
    else:
        x1, x2, x3 = -2.0 * x1, -2.0 * x2, -2.0 * x3
        parts = [x1, x1, x2, x2, x1, x3, stacked(one, one, one, n1, n2, n3), zero]
    return jnp.concatenate(parts, axis=0)


def lanes(chunk):
    if isinstance(chunk, int):
        return pl.ds(128 * chunk, 128)
    return pl.ds(pl.multiple_of(chunk * 128, 128), 128)


def put(chunk, z, v, row_side, pts, vec):
    wide = pieces(z, row_side)
    if row_side:
        pts[:, lanes(chunk)] = wide.astype(H)
    else:
        pts[lanes(chunk), :] = wide.T.astype(H)
    high = v.astype(H)
    vec[0:32, lanes(chunk)] = high
    vec[32:64, lanes(chunk)] = (v - high.astype(F)).astype(H)


def prepare(src, slots, chunk0, row_side, pts, vec):
    first, count = slots

    @pl.loop(0, count)
    def _(s):
        put(chunk0 + s, src[first + s, 0:16, :], src[first + s, 16:48, :], row_side, pts, vec)


def prepare_rest(src, slots, chunk, row_side, pts, vec):
    first, count = slots
    group_of = lax.broadcasted_iota(jnp.int32, (16, 128), 1) // 32
    outs = [jnp.zeros((16, 128), F) for _ in range(3)]
    for k in range(count):
        rem = src[first + k, 48:64, :]
        for q in range(3):
            turn = (32 * (k - q)) % 128
            outs[q] = jnp.where(group_of == k, pltpu.roll(rem, turn, 1) if turn else rem, outs[q])
    put(chunk, outs[0], jnp.concatenate(outs[1:], axis=0), row_side, pts, vec)


def finish(acc, slots, chunk0, rest, out):
    first, count = slots
    group_of = lax.broadcasted_iota(jnp.int32, (8, 128), 1) // 32
    c = lanes(rest)
    t = (acc[0:32, c] + acc[32:64, c]) * GAIN
    for k in range(count):
        c = lanes(chunk0 + k)
        out[first + k, 0:32, :] = (acc[0:32, c] + acc[32:64, c]) * GAIN
        o = jnp.zeros((8, 128), F)
        for q in range(4):
            turn = (32 * (q - k)) % 128
            piece = t[8 * q : 8 * q + 8, :]
            o = jnp.where(group_of == q, pltpu.roll(piece, turn, 1) if turn else piece, o)
        out[first + k, 32:40, :] = o


def block_of(m):
    late = m - 15
    j = jnp.where(m < 9, lax.div(m, 3), jnp.where(m < 12, m - 9, jnp.where(m < 15, m - 12, jnp.where(m < 25, 3 + lax.div(jnp.maximum(late, 0), 5), 5))))
    i = jnp.where(m < 9, lax.rem(m, 3), jnp.where(m < 12, 3, jnp.where(m < 15, 4, jnp.where(m < 25, lax.rem(jnp.maximum(late, 0), 5), 29 - m))))
    return j, i


STEPS = 30


def products(A, vj, B, vi, acc_i, acc_j, d, k, actions):
    def place(block, q):
        j, i = block
        return (
            pl.ds(pl.multiple_of((2 * j + q // 2) * TILE, TILE), TILE),
            pl.ds(pl.multiple_of((2 * i + q % 2) * TILE, TILE), TILE),
        )

    def distances(block, q):
        sj, si = place(block, q)
        d[q][...] = jnp.dot(A[sj, :], B[:, si], preferred_element_type=F)

    def kernel_values(q):
        x = jnp.maximum(d[q][...], TINY)
        u = (-ALPHA) - x * lax.rsqrt(x)
        value = (u * u + BETA) * jnp.exp2(u)
        high = value.astype(H)
        k[q][0] = high
        k[q][1] = (value - high.astype(F)).astype(H)

    def accumulate(block, q):
        sj, si = place(block, q)
        v_j, v_i = vj[:, sj], vi[:, si]
        acc_i[:, si] += jnp.dot(
            jnp.concatenate([v_j, v_j], axis=1), jnp.concatenate([k[q][0], k[q][1]], axis=0), preferred_element_type=F
        )
        acc_j[:, sj] += jnp.dot(
            jnp.concatenate([v_i, v_i], axis=1), jnp.concatenate([k[q][0].T, k[q][1].T], axis=0), preferred_element_type=F
        )

    for q in range(3):
        distances(block_of(jnp.int32(0)), q)
    for q in range(1, 4):
        k[q][...] = jnp.zeros_like(k[q])

    @pl.loop(0, STEPS)
    def _(m):
        for step, action in actions.items():
            if step < STEPS:
                pl.when(m == step)(action)
        before, now = block_of(jnp.maximum(m - 1, 0)), block_of(m)
        after = block_of(jnp.minimum(m + 1, STEPS - 1))
        for q in range(4):
            distances(after if q else now, (q + 3) % 4)
            accumulate(before if q < 3 else now, (q + 1) % 4)
            kernel_values(q)

    actions[STEPS]()
    for q in range(1, 4):
        accumulate(block_of(jnp.int32(STEPS - 1)), q)


def solve_kernel(p_hbm, v_hbm, l_ref, out_ref, p_ref, v_ref, R, C, B, vi, A, vj, acc_i, acc_j, d0, d1, d2, d3, k0, k1, k2, k3,
                 oi, oj, gi, gj, io, rs, rr, cs, cr, ris, rir, cjs, cjr):
    b, r = lax.axis_index("blk"), lax.axis_index("rep")
    core, z, x = lax.rem(b, 2), lax.div(b, 8), lax.rem(r, 4)
    y = lax.div(r, 4) * 4 + lax.rem(lax.div(b, 2), 4)

    def at(dx=0, dy=0, dz=0, dc=0):
        xx, yy, zz = lax.rem(x + dx + 4, 4), lax.rem(y + dy + 8, 8), lax.rem(z + dz + 8, 8)
        cc = 1 - core if dc else core
        return ((zz * 4 + lax.rem(yy, 4)) * 2 + cc, lax.div(yy, 4) * 4 + xx)

    barrier = pltpu.get_barrier_semaphore()
    near = [at(dc=1), at(dz=1), at(dz=-1), at(dy=1), at(dy=-1), at(dx=1), at(dx=-1)]
    for d in near:
        pl.semaphore_signal(barrier, inc=1, device_id=d, device_id_type=pl.DeviceIdType.MESH)
    loads = [pltpu.make_async_copy(p_hbm, p_ref, io.at[0]), pltpu.make_async_copy(v_hbm, v_ref, io.at[1])]
    for t in loads:
        t.start()
    feature = lax.broadcasted_iota(jnp.int32, (16, 160), 0)
    scale = jnp.ones((16, 160), F)
    for f in range(16):
        scale = jnp.where(feature == f, l_ref[f], scale)
    acc_i[...] = jnp.zeros_like(acc_i)
    acc_j[...] = jnp.zeros_like(acc_j)
    pad = pl.ds(NJ - 128, 128)
    A[pad, :] = jnp.zeros((128, 128), H)
    vj[:, pad] = jnp.zeros((64, 128), H)
    for t in loads:
        t.wait()

    own = R.at[0]
    scaled = p_ref[...] / scale * SCALE
    R[0, 0:16, :] = scaled[:, 0:128]
    R[0, 16:48, :] = v_ref[:, 0:128]
    R[0, 48:64, 0:32] = scaled[:, 128:160]
    R[0, 48:64, 32:64] = v_ref[0:16, 128:160]
    R[0, 48:64, 64:96] = v_ref[16:32, 128:160]
    R[0, 48:64, 96:128] = jnp.zeros((16, 32), F)
    C[NSYM] = R[0]
    pl.semaphore_wait(barrier, len(near))

    def send(source, dest, ss, rsem, where):
        return pltpu.make_async_remote_copy(
            src_ref=source, dst_ref=dest, send_sem=ss, recv_sem=rsem, device_id=where,
            device_id_type=pl.DeviceIdType.MESH,
        )

    row, col = {}, {}
    rslot = {dz: 2 * k for k, dz in enumerate(ROWS)}
    for dz in range(8):
        for dc in range(2):
            s = rslot[dz] + dc
            if s == 0:
                continue
            if dc:
                source, where = R.at[rslot[dz]], at(dc=1)
            elif dz <= 4:
                source, where = R.at[rslot[dz - 1]], at(dz=-1)
            else:
                source, where = R.at[rslot[(dz + 1) % 8]], at(dz=1)
            row[dz, dc] = send(source, R.at[s], rs.at[s], rr.at[s], where)
    slot = {o: k for k, o in enumerate(COLS)}
    for (dx, dy), s in slot.items():
        if (dx, dy) == (0, 0):
            continue
        if dx == 0:
            prev, where = (0, dy - 1), at(dy=-1)
        elif dx == 1:
            prev, where = (0, dy), at(dx=-1)
        elif dx == -1:
            prev, where = (0, dy), at(dx=1)
        elif dy <= 1:
            prev, where = (1, dy), at(dx=-1)
        else:
            prev, where = (-1, dy), at(dx=1)
        source = own if prev == (0, 0) else C.at[slot[prev]]
        col[dx, dy] = send(source, C.at[s], cs.at[s], cr.at[s], where)

    for t in (col[0, 1], row[1, 0], row[7, 0], col[1, 0], row[0, 1]):
        t.start()

    def arrive_row(dz, *then):
        row[dz, 0].wait_recv()
        for t in then:
            row[t, 0].start()
        row[dz, 1].start()

    def arrive_col(o, *then):
        col[o].wait_recv()
        for t in then:
            col[t].start()

    def rows_ready(*offsets):
        for dz in offsets:
            row[dz, 1].wait_recv()

    def prepare_rows(group):
        prepare(R, (4 * group, 4), 4 * group, True, B, vi)

    def prepare_cols(first, count, chunk):
        prepare(C, (first, count), chunk, False, A, vj)

    backs = {}

    def back(key, source, dest, ss, rsem, where):
        backs[key] = send(source, dest, ss, rsem, where)

    for k, (dx, dy) in enumerate(SYM):
        back((dx, dy), oj.at[k], gj.at[k], cjs.at[k], cjr.at[k], at(dx=dx, dy=dy))
    for dz in range(8):
        for dc in range(2):
            if (dz, dc) != (0, 0):
                s, d = rslot[dz] + dc, rslot[(8 - dz) % 8] + dc
                back((dz, dc, 0), oi.at[s], gi.at[d], ris.at[d], rir.at[d], at(dz=dz, dc=dc))

    def return_rows(group):
        finish(acc_i, (4 * group, 4), 4 * group, NROW + group, oi)
        for k in (2 * group + 1, 2 * group):
            for dc in range(2):
                if (ROWS[k], dc) != (0, 0):
                    backs[ROWS[k], dc, 0].start()

    def return_cols():
        for g in range(4):
            finish(acc_j, (4 * g, min(4, NSYM - 4 * g)), 4 * g, NSYM + g, oj)
        for o in SYM:
            backs[o].start()

    arrive_col((0, 1), (0, 2), (1, 1), (-1, 1))
    arrive_row(1, 2)
    arrive_row(7, 6)
    arrive_col((1, 0), (2, 0))
    arrive_col((0, 2), (0, 3), (1, 2), (-1, 2))
    arrive_row(2, 3)
    arrive_row(6, 5)
    arrive_col((1, 1), (2, 1))
    rows_ready(0, 1)
    prepare_rows(0)
    prepare_cols(0, 4, 0)
    rows_ready(7, 2)
    prepare_rows(1)

    def at_1():
        arrive_col((0, 3), (0, 4), (1, 3), (-1, 3))
        arrive_row(3, 4)
        arrive_row(5)
        rows_ready(6, 3)
        prepare_rows(2)

    def at_2():
        arrive_col((-1, 2), (2, 2))
        arrive_col((-1, 1))
        arrive_col((1, 2))
        prepare_cols(4, 4, 4)

    def at_5():
        arrive_col((0, 4), (-1, 4))
        arrive_row(4)
        arrive_col((-1, 3), (2, 3))
        arrive_col((2, 1))
        arrive_col((1, 3))
        arrive_col((2, 2))
        prepare_cols(8, 4, 8)

    def at_8():
        rows_ready(5, 4)
        prepare_rows(3)

    def at_11():
        for g in range(4):
            prepare_rest(R, (4 * g, 4), NROW + g, True, B, vi)

    def at_14():
        arrive_col((-1, 4), (2, 4))
        arrive_col((2, 3))
        prepare_cols(12, 2, 12)
        for g in range(2):
            prepare_rest(C, (4 * g, 4), NSYM + g, False, A, vj)

    def at_19():
        arrive_col((2, 0))
        for g in range(2, 4):
            prepare_rest(C, (4 * g, min(4, NSYM - 4 * g)), NSYM + g, False, A, vj)
        prepare_cols(NSYM, 2, CHUNK_S)

    def at_24():
        arrive_col((2, 4))
        prepare_cols(NSYM + 2, 2, CHUNK_S + 2)
        prepare_rest(C, (NSYM, 4), CHUNK_S + 4, False, A, vj)

    actions = {
        1: at_1, 2: at_2, 5: at_5, 8: at_8, 11: at_11, 14: at_14, 19: at_19, 24: at_24,
        26: return_cols,
        28: lambda: return_rows(3),
        29: lambda: return_rows(2),
        STEPS: lambda: return_rows(1),
    }
    products(A, vj, B, vi, acc_i, acc_j, (d0, d1, d2, d3), (k0, k1, k2, k3), actions)
    return_rows(0)

    total = oi[0]
    for k, o in enumerate(SYM):
        backs[o].wait_recv()
        total = total + gj[k]
    for dz in (*ROWS[:0:-1], 0):
        for dc in range(2):
            if (dz, dc) != (0, 0):
                backs[dz, dc, 0].wait_recv()
                total = total + gi[rslot[(8 - dz) % 8] + dc]
    out_ref[:, 0:128] = total[0:32]
    rem = total[32:40]
    for q in range(4):
        turned = pltpu.roll(rem, (-32 * q) % 128, 1) if q else rem
        out_ref[8 * q : 8 * q + 8, 128:160] = turned[:, 0:32]
    for t in (*row.values(), *col.values(), *backs.values()):
        t.wait_send()


def per_device(points, vectors, lengthscales):
    vmem = pl.BlockSpec(memory_space=pltpu.VMEM)
    dma = pltpu.SemaphoreType.DMA
    return pl.pallas_call(
        solve_kernel,
        out_shape=jax.ShapeDtypeStruct(vectors.shape, F),
        in_specs=[pl.BlockSpec(memory_space=pl.ANY)] * 2 + [pl.BlockSpec(memory_space=pltpu.SMEM)],
        out_specs=vmem,
        scratch_shapes=[
            pltpu.VMEM(points.shape, F),
            pltpu.VMEM(vectors.shape, F),
            pltpu.VMEM((NROW, 64, 128), F),
            pltpu.VMEM((NCOL, 64, 128), F),
            pltpu.VMEM((128, NI), H),
            pltpu.VMEM((64, NI), H),
            pltpu.VMEM((NJ, 128), H),
            pltpu.VMEM((64, NJ), H),
            pltpu.VMEM((64, NI), F),
            pltpu.VMEM((64, NJ), F),
            *[pltpu.VMEM((TILE, TILE), F)] * 4,
            *[pltpu.VMEM((2, TILE, TILE), H)] * 4,
            pltpu.VMEM((NROW, 40, 128), F),
            pltpu.VMEM((NSYM, 40, 128), F),
            pltpu.VMEM((NROW, 40, 128), F),
            pltpu.VMEM((NSYM, 40, 128), F),
            dma((2,)),
            dma((NROW,)), dma((NROW,)), dma((NCOL,)), dma((NCOL,)),
            dma((NROW,)), dma((NROW,)), dma((NSYM,)), dma((NSYM,)),
        ],
        compiler_params=pltpu.CompilerParams(collective_id=0, has_side_effects=True),
        name="solve",
    )(points, vectors, lengthscales)


def solution(mesh):
    return jax.shard_map(
        per_device,
        mesh=mesh,
        in_specs=(P(None, ("blk", "rep")), P(None, ("blk", "rep")), P()),
        out_specs=P(None, ("blk", "rep")),
        check_vma=False,
    )
```

time: 74.5 us -> 63.4 us (0.85); the launches traced: 73.1 us -> 63.2 us
  Pallas kernels: 70.4 us -> 61.8 us
  local copies, waits for them, and re-layouts: 2.71 us -> 1.38 us
    pallas_call x1, Pallas kernels: 70.4 us -> 61.8 us  [per_device(): pl.pallas_call(solve_kernel, out_shape=jax.ShapeDtypeStruct(vectors.shape...]
    unnamed x3 -> x1, local copies, waits for them, and re-layouts: 2.03 us -> 1.38 us
where the time goes in v2:
time: 63.4 us; the launch traced here: 63.2 us
  Pallas kernels  61.8 us (97%)
  local copies, waits for them, and re-layouts  1.38 us (2%)
    pallas_call x1, Pallas kernels, per_device(): pl.pallas_call(solve_kernel, out_shape=jax.ShapeDtypeStruct(vectors.shape...  61.8 us
    unnamed x1, local copies, waits for them, and re-layouts  1.38 us

profile of v2, /device:TPU:1, one launch (start us, length us, event | category | flops | bytes accessed | tf_op | source)
XLA Modules:
  0.0 63.2 jit_solution(12567906547495232218)
XLA Ops:
  0.0 61.8 %solve.1 = f32[32,160]{1,0:T(8,128)} custom-call(f32[16,160]{1,0:T(8,128)} %p_hbm.1, f32[32,160]{1,0:T(8,128)} %v_hbm.1, f32[16]{0:T(128)} %l_ref.1), custom_call_target="tpu_custom_call" | custom-call | tf_op jit(solution)/shard_map/solve/pallas_call | solution.py:393
  61.8 1.4 %copy.5 = f32[32,160]{1,0:T(8,128)} copy(f32[32,160]{1,0:T(8,128)} %solve.1) | data formatting | bytes 40960

commit v3 on v2

--- a/solution.py
+++ b/solution.py
@@ -18,7 +18,7 @@
 TILE = 256
 
 ROWS = [0, 1, 7, 2, 6, 3, 5, 4]
-SYM = [(0, 1), (1, 0), (0, 2), (1, 1), (-1, 1), (0, 3), (1, 2), (-1, 2), (2, 1), (1, 3), (-1, 3), (2, 2), (2, 3), (-1, 4)]
+SYM = [(0, 1), (1, 0), (0, 2), (0, 3), (1, 1), (-1, 1), (1, 2), (-1, 2), (2, 1), (2, 2), (1, 3), (-1, 3), (2, 3), (-1, 4)]
 OWN = [(0, 0), (2, 0), (0, 4), (2, 4)]
 COLS = SYM + OWN
 NROW, NCOL, NSYM = 16, len(COLS), len(SYM)
@@ -91,14 +91,19 @@
     put(chunk, outs[0], jnp.concatenate(outs[1:], axis=0), row_side, pts, vec)
 
 
-def finish(acc, slots, chunk0, rest, out):
+def finish_main(acc, slots, chunk0, out):
+    first, count = slots
+    for k in range(count):
+        c = lanes(chunk0 + k)
+        out[first + k, 0:32, :] = (acc[0:32, c] + acc[32:64, c]) * GAIN
+
+
+def finish_rest(acc, slots, rest, out):
     first, count = slots
     group_of = lax.broadcasted_iota(jnp.int32, (8, 128), 1) // 32
     c = lanes(rest)
     t = (acc[0:32, c] + acc[32:64, c]) * GAIN
     for k in range(count):
-        c = lanes(chunk0 + k)
-        out[first + k, 0:32, :] = (acc[0:32, c] + acc[32:64, c]) * GAIN
         o = jnp.zeros((8, 128), F)
         for q in range(4):
             turn = (32 * (q - k)) % 128
@@ -108,9 +113,13 @@
 
 
 def block_of(m):
-    late = m - 15
-    j = jnp.where(m < 9, lax.div(m, 3), jnp.where(m < 12, m - 9, jnp.where(m < 15, m - 12, jnp.where(m < 25, 3 + lax.div(jnp.maximum(late, 0), 5), 5))))
-    i = jnp.where(m < 9, lax.rem(m, 3), jnp.where(m < 12, 3, jnp.where(m < 15, 4, jnp.where(m < 25, lax.rem(jnp.maximum(late, 0), 5), 29 - m))))
+    def pick(cond, yes, no):
+        return jnp.where(cond, yes, no)
+
+    third = pick(m >= 6, 2, pick(m >= 3, 1, 0))
+    pair = lax.shift_right_logical(jnp.maximum(m - 20, 0), 1)
+    j = pick(m < 9, third, pick(m < 12, m - 9, pick(m < 15, m - 12, pick(m < 20, 3, m - 16 - 2 * pair))))
+    i = pick(m < 9, m - 3 * third, pick(m < 12, 3, pick(m < 15, 4, pick(m < 20, m - 15, 4 - pair))))
     return j, i
 
 
@@ -152,18 +161,19 @@
     for q in range(1, 4):
         k[q][...] = jnp.zeros_like(k[q])
 
-    @pl.loop(0, STEPS)
-    def _(m):
-        for step, action in actions.items():
-            if step < STEPS:
-                pl.when(m == step)(action)
-        before, now = block_of(jnp.maximum(m - 1, 0)), block_of(m)
-        after = block_of(jnp.minimum(m + 1, STEPS - 1))
+    def step(m, blocks):
+        for at, action in actions.items():
+            if at < STEPS:
+                pl.when(m == at)(action)
+        before, now, after = blocks
         for q in range(4):
             distances(after if q else now, (q + 3) % 4)
             accumulate(before if q < 3 else now, (q + 1) % 4)
             kernel_values(q)
-
+        return now, after, block_of(jnp.minimum(m + 2, STEPS - 1))
+
+    start = block_of(jnp.int32(0))
+    lax.fori_loop(0, STEPS, step, (start, start, block_of(jnp.int32(1))))
     actions[STEPS]()
     for q in range(1, 4):
         accumulate(block_of(jnp.int32(STEPS - 1)), q)
@@ -181,7 +191,7 @@
         return ((zz * 4 + lax.rem(yy, 4)) * 2 + cc, lax.div(yy, 4) * 4 + xx)
 
     barrier = pltpu.get_barrier_semaphore()
-    near = [at(dc=1), at(dz=1), at(dz=-1), at(dy=1), at(dy=-1), at(dx=1), at(dx=-1)]
+    near = [at(dc=1)] + [at(dz=k) for k in range(1, 8)] + [at(dy=k) for k in range(1, 8)] + [at(dx=k) for k in range(1, 4)]
     for d in near:
         pl.semaphore_signal(barrier, inc=1, device_id=d, device_id_type=pl.DeviceIdType.MESH)
     loads = [pltpu.make_async_copy(p_hbm, p_ref, io.at[0]), pltpu.make_async_copy(v_hbm, v_ref, io.at[1])]
@@ -225,29 +235,22 @@
                 continue
             if dc:
                 source, where = R.at[rslot[dz]], at(dc=1)
-            elif dz <= 4:
-                source, where = R.at[rslot[dz - 1]], at(dz=-1)
             else:
-                source, where = R.at[rslot[(dz + 1) % 8]], at(dz=1)
+                source, where = own, at(dz=-dz)
             row[dz, dc] = send(source, R.at[s], rs.at[s], rr.at[s], where)
     slot = {o: k for k, o in enumerate(COLS)}
     for (dx, dy), s in slot.items():
         if (dx, dy) == (0, 0):
             continue
         if dx == 0:
-            prev, where = (0, dy - 1), at(dy=-1)
-        elif dx == 1:
-            prev, where = (0, dy), at(dx=-1)
-        elif dx == -1:
-            prev, where = (0, dy), at(dx=1)
-        elif dy <= 1:
-            prev, where = (1, dy), at(dx=-1)
+            prev, where = (0, 0), at(dy=-dy)
         else:
-            prev, where = (-1, dy), at(dx=1)
+            prev, where = (0, dy), at(dx=-dx)
         source = own if prev == (0, 0) else C.at[slot[prev]]
         col[dx, dy] = send(source, C.at[s], cs.at[s], cr.at[s], where)
 
-    for t in (col[0, 1], row[1, 0], row[7, 0], col[1, 0], row[0, 1]):
+    for t in (col[0, 1], row[1, 0], row[7, 0], col[1, 0], row[0, 1], col[0, 2], row[2, 0], row[6, 0], col[2, 0],
+              col[0, 3], row[3, 0], row[5, 0], col[0, 4], row[4, 0]):
         t.start()
 
     def arrive_row(dz, *then):
@@ -277,34 +280,53 @@
         backs[key] = send(source, dest, ss, rsem, where)
 
     for k, (dx, dy) in enumerate(SYM):
-        back((dx, dy), oj.at[k], gj.at[k], cjs.at[k], cjr.at[k], at(dx=dx, dy=dy))
+        for part, rows in enumerate((pl.ds(0, 32), pl.ds(32, 8))):
+            e = 2 * k + part
+            back((dx, dy, part), oj.at[k, rows], gj.at[k, rows], cjs.at[e], cjr.at[e], at(dx=dx, dy=dy))
     for dz in range(8):
         for dc in range(2):
             if (dz, dc) != (0, 0):
                 s, d = rslot[dz] + dc, rslot[(8 - dz) % 8] + dc
-                back((dz, dc, 0), oi.at[s], gi.at[d], ris.at[d], rir.at[d], at(dz=dz, dc=dc))
+                back((dz, dc), oi.at[s], gi.at[d], ris.at[d], rir.at[d], at(dz=dz, dc=dc))
 
     def return_rows(group):
-        finish(acc_i, (4 * group, 4), 4 * group, NROW + group, oi)
+        finish_main(acc_i, (4 * group, 4), 4 * group, oi)
+        finish_rest(acc_i, (4 * group, 4), NROW + group, oi)
         for k in (2 * group + 1, 2 * group):
             for dc in range(2):
                 if (ROWS[k], dc) != (0, 0):
-                    backs[ROWS[k], dc, 0].start()
-
-    def return_cols():
-        for g in range(4):
-            finish(acc_j, (4 * g, min(4, NSYM - 4 * g)), 4 * g, NSYM + g, oj)
-        for o in SYM:
-            backs[o].start()
-
-    arrive_col((0, 1), (0, 2), (1, 1), (-1, 1))
-    arrive_row(1, 2)
-    arrive_row(7, 6)
-    arrive_col((1, 0), (2, 0))
-    arrive_col((0, 2), (0, 3), (1, 2), (-1, 2))
-    arrive_row(2, 3)
-    arrive_row(6, 5)
-    arrive_col((1, 1), (2, 1))
+                    backs[ROWS[k], dc].start()
+
+    def return_cols(part, first, count):
+        for o in SYM[first : first + count]:
+            backs[(*o, part)].start()
+
+    def cols_main():
+        finish_main(acc_j, (0, 12), 0, oj)
+        return_cols(0, 0, 12)
+
+    def cols_next():
+        finish_main(acc_j, (12, 2), 12, oj)
+        for g in range(2):
+            finish_rest(acc_j, (4 * g, 4), NSYM + g, oj)
+        return_cols(0, 12, 2)
+        return_cols(1, 0, 8)
+
+    def cols_last():
+        for g in range(2, 4):
+            finish_rest(acc_j, (4 * g, min(4, NSYM - 4 * g)), NSYM + g, oj)
+        return_cols(1, 8, NSYM - 8)
+
+    arrive_col((0, 1), (1, 1), (-1, 1), (2, 1))
+    arrive_row(1)
+    arrive_row(7)
+    arrive_col((0, 2), (1, 2), (-1, 2), (2, 2))
+    arrive_row(2)
+    arrive_row(6)
+    arrive_col((0, 3), (1, 3), (-1, 3), (2, 3))
+    arrive_row(3)
+    arrive_row(5)
+    arrive_col((1, 0))
     rows_ready(0, 1)
     prepare_rows(0)
     prepare_cols(0, 4, 0)
@@ -312,25 +334,19 @@
     prepare_rows(1)
 
     def at_1():
-        arrive_col((0, 3), (0, 4), (1, 3), (-1, 3))
-        arrive_row(3, 4)
-        arrive_row(5)
+        arrive_col((0, 4), (-1, 4), (2, 4))
+        arrive_row(4)
         rows_ready(6, 3)
         prepare_rows(2)
 
     def at_2():
-        arrive_col((-1, 2), (2, 2))
-        arrive_col((-1, 1))
-        arrive_col((1, 2))
+        for o in SYM[4:8]:
+            arrive_col(o)
         prepare_cols(4, 4, 4)
 
     def at_5():
-        arrive_col((0, 4), (-1, 4))
-        arrive_row(4)
-        arrive_col((-1, 3), (2, 3))
-        arrive_col((2, 1))
-        arrive_col((1, 3))
-        arrive_col((2, 2))
+        for o in SYM[8:12]:
+            arrive_col(o)
         prepare_cols(8, 4, 8)
 
     def at_8():
@@ -342,8 +358,8 @@
             prepare_rest(R, (4 * g, 4), NROW + g, True, B, vi)
 
     def at_14():
-        arrive_col((-1, 4), (2, 4))
         arrive_col((2, 3))
+        arrive_col((-1, 4))
         prepare_cols(12, 2, 12)
         for g in range(2):
             prepare_rest(C, (4 * g, 4), NSYM + g, False, A, vj)
@@ -354,29 +370,30 @@
             prepare_rest(C, (4 * g, min(4, NSYM - 4 * g)), NSYM + g, False, A, vj)
         prepare_cols(NSYM, 2, CHUNK_S)
 
-    def at_24():
+    def at_20():
         arrive_col((2, 4))
         prepare_cols(NSYM + 2, 2, CHUNK_S + 2)
         prepare_rest(C, (NSYM, 4), CHUNK_S + 4, False, A, vj)
 
     actions = {
-        1: at_1, 2: at_2, 5: at_5, 8: at_8, 11: at_11, 14: at_14, 19: at_19, 24: at_24,
-        26: return_cols,
-        28: lambda: return_rows(3),
-        29: lambda: return_rows(2),
-        STEPS: lambda: return_rows(1),
+        1: at_1, 2: at_2, 5: at_5, 8: at_8, 11: at_11, 14: at_14, 16: cols_main, 19: at_19, 20: at_20, 21: cols_next,
+        25: lambda: return_rows(3),
+        27: lambda: return_rows(2),
+        29: lambda: return_rows(1),
+        STEPS: cols_last,
     }
     products(A, vj, B, vi, acc_i, acc_j, (d0, d1, d2, d3), (k0, k1, k2, k3), actions)
     return_rows(0)
 
     total = oi[0]
     for k, o in enumerate(SYM):
-        backs[o].wait_recv()
+        backs[(*o, 0)].wait_recv()
+        backs[(*o, 1)].wait_recv()
         total = total + gj[k]
     for dz in (*ROWS[:0:-1], 0):
         for dc in range(2):
             if (dz, dc) != (0, 0):
-                backs[dz, dc, 0].wait_recv()
+                backs[dz, dc].wait_recv()
                 total = total + gi[rslot[(8 - dz) % 8] + dc]
     out_ref[:, 0:128] = total[0:32]
     rem = total[32:40]
@@ -414,7 +431,7 @@
             pltpu.VMEM((NSYM, 40, 128), F),
             dma((2,)),
             dma((NROW,)), dma((NROW,)), dma((NCOL,)), dma((NCOL,)),
-            dma((NROW,)), dma((NROW,)), dma((NSYM,)), dma((NSYM,)),
+            dma((NROW,)), dma((NROW,)), dma((2 * NSYM,)), dma((2 * NSYM,)),
         ],
         compiler_params=pltpu.CompilerParams(collective_id=0, has_side_effects=True),
         name="solve",

time: 63.4 us -> 57.8 us (0.912)
  Pallas kernels: 61.8 us -> 56.1 us
    pallas_call x1, Pallas kernels: 61.8 us -> 56.1 us  [per_device(): pl.pallas_call(solve_kernel, out_shape=jax.ShapeDtypeStruct(vectors.shape...]
where the time goes in v3:
time: 57.8 us; the launch traced here: 57.5 us
  Pallas kernels  56.1 us (97%)
  local copies, waits for them, and re-layouts  1.38 us (2%)
    pallas_call x1, Pallas kernels, per_device(): pl.pallas_call(solve_kernel, out_shape=jax.ShapeDtypeStruct(vectors.shape...  56.1 us
    unnamed x1, local copies, waits for them, and re-layouts  1.38 us

profile of v3, /device:TPU:1, one launch (start us, length us, event | category | flops | bytes accessed | tf_op | source)
XLA Modules:
  0.0 57.5 jit_solution(15443244498408879726)
XLA Ops:
  0.0 56.1 %solve.1 = f32[32,160]{1,0:T(8,128)} custom-call(f32[16,160]{1,0:T(8,128)} %p_hbm.1, f32[32,160]{1,0:T(8,128)} %v_hbm.1, f32[16]{0:T(128)} %l_ref.1), custom_call_target="tpu_custom_call" | custom-call | tf_op jit(solution)/shard_map/solve/pallas_call | solution.py:410
  56.2 1.4 %copy.5 = f32[32,160]{1,0:T(8,128)} copy(f32[32,160]{1,0:T(8,128)} %solve.1) | data formatting | bytes 40960

commit v4 on v3

--- a/solution.py
+++ b/solution.py
@@ -117,9 +117,10 @@
         return jnp.where(cond, yes, no)
 
     third = pick(m >= 6, 2, pick(m >= 3, 1, 0))
-    pair = lax.shift_right_logical(jnp.maximum(m - 20, 0), 1)
-    j = pick(m < 9, third, pick(m < 12, m - 9, pick(m < 15, m - 12, pick(m < 20, 3, m - 16 - 2 * pair))))
-    i = pick(m < 9, m - 3 * third, pick(m < 12, 3, pick(m < 15, 4, pick(m < 20, m - 15, 4 - pair))))
+    tail = m - 15
+    fifth = pick(m >= 27, 4, pick(m >= 24, 3, pick(m >= 21, 2, pick(m >= 18, 1, 0))))
+    j = pick(m < 9, third, pick(m < 12, m - 9, pick(m < 15, m - 12, 3 + tail - 3 * fifth)))
+    i = pick(m < 9, m - 3 * third, pick(m < 12, 3, pick(m < 15, 4, 4 - fifth)))
     return j, i
 
 
@@ -305,6 +306,10 @@
         finish_main(acc_j, (0, 12), 0, oj)
         return_cols(0, 0, 12)
 
+    def at_16():
+        own_rest()
+        cols_main()
+
     def cols_next():
         finish_main(acc_j, (12, 2), 12, oj)
         for g in range(2):
@@ -364,22 +369,23 @@
         for g in range(2):
             prepare_rest(C, (4 * g, 4), NSYM + g, False, A, vj)
 
-    def at_19():
+    def at_15():
         arrive_col((2, 0))
         for g in range(2, 4):
             prepare_rest(C, (4 * g, min(4, NSYM - 4 * g)), NSYM + g, False, A, vj)
         prepare_cols(NSYM, 2, CHUNK_S)
 
-    def at_20():
+    def own_rest():
         arrive_col((2, 4))
         prepare_cols(NSYM + 2, 2, CHUNK_S + 2)
         prepare_rest(C, (NSYM, 4), CHUNK_S + 4, False, A, vj)
 
     actions = {
-        1: at_1, 2: at_2, 5: at_5, 8: at_8, 11: at_11, 14: at_14, 16: cols_main, 19: at_19, 20: at_20, 21: cols_next,
-        25: lambda: return_rows(3),
-        27: lambda: return_rows(2),
-        29: lambda: return_rows(1),
+        1: at_1, 2: at_2, 5: at_5, 8: at_8, 11: at_11, 14: at_14, 15: at_15, 16: at_16,
+        22: lambda: return_rows(3),
+        25: lambda: return_rows(2),
+        28: lambda: return_rows(1),
+        29: cols_next,
         STEPS: cols_last,
     }
     products(A, vj, B, vi, acc_i, acc_j, (d0, d1, d2, d3), (k0, k1, k2, k3), actions)

time: 57.8 us -> 59.5 us (1.029)
  Pallas kernels: 56.1 us -> 57.9 us
    pallas_call x1, Pallas kernels: 56.1 us -> 57.9 us  [per_device(): pl.pallas_call(solve_kernel, out_shape=jax.ShapeDtypeStruct(vectors.shape...]
where the time goes in v4:
time: 59.5 us; the launch traced here: 59.3 us
  Pallas kernels  57.9 us (97%)
  local copies, waits for them, and re-layouts  1.38 us (2%)
    pallas_call x1, Pallas kernels, per_device(): pl.pallas_call(solve_kernel, out_shape=jax.ShapeDtypeStruct(vectors.shape...  57.9 us
    unnamed x1, local copies, waits for them, and re-layouts  1.38 us

profile of v4, /device:TPU:1, one launch (start us, length us, event | category | flops | bytes accessed | tf_op | source)
XLA Modules:
  0.0 59.3 jit_solution(14965018964317519081)
XLA Ops:
  0.0 57.9 %solve.1 = f32[32,160]{1,0:T(8,128)} custom-call(f32[16,160]{1,0:T(8,128)} %p_hbm.1, f32[32,160]{1,0:T(8,128)} %v_hbm.1, f32[16]{0:T(128)} %l_ref.1), custom_call_target="tpu_custom_call" | custom-call | tf_op jit(solution)/shard_map/solve/pallas_call | solution.py:416
  57.9 1.4 %copy.5 = f32[32,160]{1,0:T(8,128)} copy(f32[32,160]{1,0:T(8,128)} %solve.1) | data formatting | bytes 40960

commit v5 on v3

--- a/solution.py
+++ b/solution.py
@@ -23,6 +23,7 @@
 COLS = SYM + OWN
 NROW, NCOL, NSYM = 16, len(COLS), len(SYM)
 CHUNK_S = NSYM + -(-NSYM // 4)
+REST = [(6, 4), (10, 4), (0, 4), (4, 2)]
 NI, NJ = 128 * (NROW + NROW // 4), 128 * 24
 
 
@@ -308,14 +309,14 @@
     def cols_next():
         finish_main(acc_j, (12, 2), 12, oj)
         for g in range(2):
-            finish_rest(acc_j, (4 * g, 4), NSYM + g, oj)
+            finish_rest(acc_j, REST[g], NSYM + g, oj)
         return_cols(0, 12, 2)
-        return_cols(1, 0, 8)
+        return_cols(1, 6, 8)
 
     def cols_last():
         for g in range(2, 4):
-            finish_rest(acc_j, (4 * g, min(4, NSYM - 4 * g)), NSYM + g, oj)
-        return_cols(1, 8, NSYM - 8)
+            finish_rest(acc_j, REST[g], NSYM + g, oj)
+        return_cols(1, 0, 6)
 
     arrive_col((0, 1), (1, 1), (-1, 1), (2, 1))
     arrive_row(1)
@@ -362,12 +363,12 @@
         arrive_col((-1, 4))
         prepare_cols(12, 2, 12)
         for g in range(2):
-            prepare_rest(C, (4 * g, 4), NSYM + g, False, A, vj)
+            prepare_rest(C, REST[g], NSYM + g, False, A, vj)
 
     def at_19():
         arrive_col((2, 0))
         for g in range(2, 4):
-            prepare_rest(C, (4 * g, min(4, NSYM - 4 * g)), NSYM + g, False, A, vj)
+            prepare_rest(C, REST[g], NSYM + g, False, A, vj)
         prepare_cols(NSYM, 2, CHUNK_S)
 
     def at_20():

time: 57.8 us -> 57.6 us (level)
  no operation moved by 1% of the time
where the time goes in v5:
time: 57.6 us; the launch traced here: 57.3 us
  Pallas kernels  55.9 us (97%)
  local copies, waits for them, and re-layouts  1.38 us (2%)
    pallas_call x1, Pallas kernels, per_device(): pl.pallas_call(solve_kernel, out_shape=jax.ShapeDtypeStruct(vectors.shape...  55.9 us
    unnamed x1, local copies, waits for them, and re-layouts  1.38 us

profile of v5, /device:TPU:1, one launch (start us, length us, event | category | flops | bytes accessed | tf_op | source)
XLA Modules:
  0.0 57.3 jit_solution(16448826690942291191)
XLA Ops:
  0.0 55.9 %solve.1 = f32[32,160]{1,0:T(8,128)} custom-call(f32[16,160]{1,0:T(8,128)} %p_hbm.1, f32[32,160]{1,0:T(8,128)} %v_hbm.1, f32[16]{0:T(128)} %l_ref.1), custom_call_target="tpu_custom_call" | custom-call | tf_op jit(solution)/shard_map/solve/pallas_call | solution.py:411
  55.9 1.4 %copy.5 = f32[32,160]{1,0:T(8,128)} copy(f32[32,160]{1,0:T(8,128)} %solve.1) | data formatting | bytes 40960

commit v6 on v5

--- a/solution.py
+++ b/solution.py
@@ -236,6 +236,8 @@
                 continue
             if dc:
                 source, where = R.at[rslot[dz]], at(dc=1)
+            elif dz == 4:
+                source, where = R.at[rslot[3]], at(dz=-1)
             else:
                 source, where = own, at(dz=-dz)
             row[dz, dc] = send(source, R.at[s], rs.at[s], rr.at[s], where)
@@ -244,14 +246,14 @@
         if (dx, dy) == (0, 0):
             continue
         if dx == 0:
-            prev, where = (0, 0), at(dy=-dy)
+            prev, where = ((0, 3), at(dy=-1)) if dy == 4 else ((0, 0), at(dy=-dy))
         else:
             prev, where = (0, dy), at(dx=-dx)
         source = own if prev == (0, 0) else C.at[slot[prev]]
         col[dx, dy] = send(source, C.at[s], cs.at[s], cr.at[s], where)
 
     for t in (col[0, 1], row[1, 0], row[7, 0], col[1, 0], row[0, 1], col[0, 2], row[2, 0], row[6, 0], col[2, 0],
-              col[0, 3], row[3, 0], row[5, 0], col[0, 4], row[4, 0]):
+              col[0, 3], row[3, 0], row[5, 0]):
         t.start()
 
     def arrive_row(dz, *then):
@@ -324,8 +326,8 @@
     arrive_col((0, 2), (1, 2), (-1, 2), (2, 2))
     arrive_row(2)
     arrive_row(6)
-    arrive_col((0, 3), (1, 3), (-1, 3), (2, 3))
-    arrive_row(3)
+    arrive_col((0, 3), (0, 4), (1, 3), (-1, 3), (2, 3))
+    arrive_row(3, 4)
     arrive_row(5)
     arrive_col((1, 0))
     rows_ready(0, 1)
@@ -335,8 +337,6 @@
     prepare_rows(1)
 
     def at_1():
-        arrive_col((0, 4), (-1, 4), (2, 4))
-        arrive_row(4)
         rows_ready(6, 3)
         prepare_rows(2)
 
@@ -346,6 +346,8 @@
         prepare_cols(4, 4, 4)
 
     def at_5():
+        arrive_col((0, 4), (-1, 4), (2, 4))
+        arrive_row(4)
         for o in SYM[8:12]:
             arrive_col(o)
         prepare_cols(8, 4, 8)

time: 57.6 us -> 56.9 us (0.988)
  Pallas kernels: 55.9 us -> 55.2 us
    pallas_call x1, Pallas kernels: 55.9 us -> 55.2 us  [per_device(): pl.pallas_call(solve_kernel, out_shape=jax.ShapeDtypeStruct(vectors.shape...]
where the time goes in v6:
time: 56.9 us; the launch traced here: 56.6 us
  Pallas kernels  55.2 us (97%)
  local copies, waits for them, and re-layouts  1.38 us (2%)
    pallas_call x1, Pallas kernels, per_device(): pl.pallas_call(solve_kernel, out_shape=jax.ShapeDtypeStruct(vectors.shape...  55.2 us
    unnamed x1, local copies, waits for them, and re-layouts  1.38 us

profile of v6, /device:TPU:1, one launch (start us, length us, event | category | flops | bytes accessed | tf_op | source)
XLA Modules:
  0.0 56.6 jit_solution(2591566636372615734)
XLA Ops:
  0.0 55.2 %solve.1 = f32[32,160]{1,0:T(8,128)} custom-call(f32[16,160]{1,0:T(8,128)} %p_hbm.1, f32[32,160]{1,0:T(8,128)} %v_hbm.1, f32[16]{0:T(128)} %l_ref.1), custom_call_target="tpu_custom_call" | custom-call | tf_op jit(solution)/shard_map/solve/pallas_call | solution.py:413
  55.2 1.4 %copy.5 = f32[32,160]{1,0:T(8,128)} copy(f32[32,160]{1,0:T(8,128)} %solve.1) | data formatting | bytes 40960
